TPU v7x, 256 devices: a whole 4x4x8 slice. The times are simulated.
256 devices in a mesh: blk: 32 (over y_lo, z, core), frq: 8 (over y_hi, x).
Axes of the slice: x: 4, y: 4 (y_hi: 2, y_lo: 2; y = y_hi * 2 + y_lo), z: 8, core: 2. Of those that a mesh axis runs over, the one named last changes fastest.
Arguments:
- spectra: bfloat16 [2, 8192, 4, 2048], P(None, 'blk', None, 'frq'), may hold values from -6 to 6
- channel_valid: int32 [8192], P('blk'), may hold values 0 or 1
Outputs:
- stacked: float32 [32, 4, 201, 256], P('blk', None, None, 'frq')
Inputs may be any that keep to these rules, and one draw needn't show every extreme that they name: `channel_valid`: 1 marks a usable channel.
All inputs are finite; a program needn't handle non-finite values. No bound on the sum of `channel_valid` on one device may be relied on, other than what follows from the above.
Results may differ from a plain program's by a relative error of at most 0.006.
Values may be sent and summed in bfloat16 or wider, within the bound.
A program may use at most 128 MiB of HBM per device.

v0:
```python
import math

import jax
import jax.numpy as jnp
from jax import lax
from jax.sharding import PartitionSpec as P

LAGS = 201
ROUNDS = 4


def from_behind(value, axis, steps):
    count = lax.axis_size(axis)
    first, last = (max(0, -steps), min(count, count - steps))
    return lax.ppermute(value, axis, [(source, source + steps) for source in range(first, last)])


def matmul_high(left, right):
    return jnp.dot(left, right, precision=lax.Precision.HIGHEST, preferred_element_type=jnp.float32)


def angle_table(first_index, second_index, period):
    product = jnp.mod(first_index[:, None] * second_index[None, :], period)
    return 2.0 * math.pi / period * product.astype(jnp.float32)


def split_table(table):
    upper = table.astype(jnp.bfloat16)
    lower = (table - upper.astype(jnp.float32)).astype(jnp.bfloat16)
    return (upper, lower)


def twiddle_product(pair, data):
    return jnp.dot(pair[0], data, preferred_element_type=jnp.float32) + jnp.dot(
        pair[1], data, preferred_element_type=jnp.float32
    )


def to_wavenumber(spectrum_in, cos_pair, sin_pair):
    channels = spectrum_in.shape[1]
    flattened = spectrum_in.reshape(2, channels, -1)
    real_part = twiddle_product(cos_pair, flattened[0]) + twiddle_product(sin_pair, flattened[1])
    imag_part = twiddle_product(cos_pair, flattened[1]) - twiddle_product(sin_pair, flattened[0])
    return jnp.stack([real_part, imag_part])


def lag_terms(own_hat, far_hat, windows, inv_cos, inv_sin, lag_cos, lag_sin, normalizer):
    length = own_hat.shape[1]
    own_hat = own_hat.reshape(2, length, windows, -1)
    far_hat = far_hat.reshape(2, length, windows, -1)
    cross_real = jnp.sum(own_hat[0] * far_hat[0] + own_hat[1] * far_hat[1], axis=1)
    cross_imag = jnp.sum(own_hat[1] * far_hat[0] - own_hat[0] * far_hat[1], axis=1)
    stack_real = matmul_high(inv_cos, cross_real) - matmul_high(inv_sin, cross_imag)
    stack_imag = matmul_high(inv_sin, cross_real) + matmul_high(inv_cos, cross_imag)
    return normalizer * (matmul_high(lag_cos, stack_real.T) - matmul_high(lag_sin, stack_imag.T))


def on_device(spectra, channel_valid):
    channels = spectra.shape[1]
    windows = spectra.shape[2]
    freq_local = spectra.shape[3]
    spectra_f = spectra.astype(jnp.float32)
    mean_power = jnp.mean(
        spectra_f[0] * spectra_f[0] + spectra_f[1] * spectra_f[1], axis=1, keepdims=True
    )
    whiten_scale = channel_valid.astype(jnp.float32)[:, None, None] / jnp.maximum(
        jnp.sqrt(mean_power), 0.5
    )
    whitened = (spectra_f * whiten_scale[None]).astype(jnp.bfloat16)
    length = 2 * channels
    chan_index = jnp.arange(channels, dtype=jnp.int32)
    wave_index = jnp.arange(length, dtype=jnp.int32)
    fwd_angle = angle_table(wave_index, chan_index, length)
    cos_pair = split_table(jnp.cos(fwd_angle))
    sin_pair = split_table(jnp.sin(fwd_angle))
    inv_angle = angle_table(chan_index - channels // 2, wave_index, length)
    inv_cos, inv_sin = (jnp.cos(inv_angle) / length, jnp.sin(inv_angle) / length)
    freq_total = freq_local * lax.axis_size("frq")
    freq_start = lax.axis_index("frq") * freq_local
    lag_index = jnp.arange(LAGS, dtype=jnp.int32) - (LAGS - 1) // 2
    freq_index = freq_start + jnp.arange(freq_local, dtype=jnp.int32)
    lag_angle = angle_table(lag_index, freq_index, 2 * freq_total)
    lag_cos, lag_sin = (jnp.cos(lag_angle), jnp.sin(lag_angle))
    normalizer = 1.0 / math.sqrt(windows * channels * freq_total)
    own_hat = to_wavenumber(whitened, cos_pair, sin_pair)
    partials = []
    for distance in range(1, ROUNDS + 1):
        far_raw = from_behind(whitened, "blk", distance)
        far_hat = to_wavenumber(far_raw, cos_pair, sin_pair)
        partial_term = lag_terms(
            own_hat, far_hat, windows, inv_cos, inv_sin, lag_cos, lag_sin, normalizer
        )
        partials.append(lax.psum_scatter(partial_term, "frq", scatter_dimension=1, tiled=True))
    stacked = jnp.stack(partials)
    return stacked[None]


def solution(mesh):
    return jax.shard_map(
        on_device,
        mesh=mesh,
        in_specs=(P(None, "blk", None, "frq"), P("blk")),
        out_specs=P("blk", None, None, "frq"),
        check_vma=False,
    )
```

profile of v0, /device:TPU:1, one launch (start us, length us, event | category | flops | bytes accessed | tf_op | source)
XLA Modules:
  0.0 576.9 jit_solution(12120927895303963031)
XLA Ops:
  9.7 6.7 %collective-permute-start.3 = (bf16[2,256,4,256]{3,2,1,0:T(4,128)(2,1)S(1)}, bf16[2,256,4,256]{3,2,1,0:T(4,128)(2,1)}, u32[]{:S(2)}, u32[]{:S(2)}) collective-permute-start(bf16[2,256,4,256]{3,2,1,0:T(4,128)(2,1)S(1)} %multiply_convert_fusion), channel_id=1, source_target_pairs={{0,32},{8,40},{16,48},{24,56},{32,64},{40,72},{48,80},{56,88},{64,... | collective-permute-start | bytes 3145736 | tf_op jit(solution)/shard_map/ppermute | solution.py:15
  16.4 7.0 %collective-permute-start.2 = (bf16[2,256,4,256]{3,2,1,0:T(4,128)(2,1)S(1)}, bf16[2,256,4,256]{3,2,1,0:T(4,128)(2,1)}, u32[]{:S(2)}, u32[]{:S(2)}) collective-permute-start(bf16[2,256,4,256]{3,2,1,0:T(4,128)(2,1)S(1)} %multiply_convert_fusion), channel_id=1, source_target_pairs={{0,24},{8,32},{16,40},{24,48},{32,56},{40,64},{48,72},{56,80},{64,... | collective-permute-start | bytes 3145736 | tf_op jit(solution)/shard_map/ppermute | solution.py:15
  30.7 3.4 fusion.48
  34.2 3.4 fusion.59
  37.6 3.4 fusion.39
  41.0 3.4 fusion.50
  44.5 4.6 fusion.62
  49.1 3.9 add_subtract_fusion.4
  54.7 36.8 %collective-permute-done.2 = bf16[2,256,4,256]{3,2,1,0:T(4,128)(2,1)} collective-permute-done((bf16[2,256,4,256]{3,2,1,0:T(4,128)(2,1)S(1)}, bf16[2,256,4,256]{3,2,1,0:T(4,128)(2,1)}, u32[]{:S(2)}, u32[]{:S(2)}) %collective-permute-start.2) | collective-permute-done | bytes 1048608 | tf_op jit(solution)/shard_map/ppermute | solution.py:15
  97.7 18.3 %collective-permute-done.1 = bf16[2,256,4,256]{3,2,1,0:T(4,128)(2,1)} collective-permute-done((bf16[2,256,4,256]{3,2,1,0:T(4,128)(2,1)S(1)}, bf16[2,256,4,256]{3,2,1,0:T(4,128)(2,1)}, u32[]{:S(2)}, u32[]{:S(2)}) %collective-permute-start.1) | collective-permute-done | bytes 1048608 | tf_op jit(solution)/shard_map/ppermute | solution.py:15
  143.9 3.4 fusion.67
  154.2 3.8 fusion.69
  164.9 3.4 fusion.71
  170.6 3.4 fusion.47
  174.0 3.6 fusion.70
  179.9 3.9 add_add_fusion.1
  191.0 3.5 add_subtract_fusion.1
  194.5 3.4 add_subtract_fusion.2
  197.9 3.5 add_subtract_fusion.3
  201.4 11.0 %multiply_subtract_fusion.3 = (f32[512,1024]{1,0:T(8,128)}, f32[512,1024]{1,0:T(8,128)}, f32[512,1024]{1,0:T(8,128)}, f32[512,1024]{1,0:T(8,128)}, f32[512,1024]...) fusion(f32[512,1024]{1,0:T(8,128)} %add_subtract_fusion.3, ...), kind=kOutput, calls=%fused_computation.12 | convolution fusion | flops 284950528 | bytes 42467328 | tf_op jit(solution)/shard_map/dot_general | solution.py:34
  225.3 3.6 fusion.78
  228.9 3.6 fusion.74
  236.1 3.6 fusion.77
  239.7 3.6 fusion.73
  275.3 3.6 fusion.76
  282.8 3.0 fusion.2
  285.8 4.1 convolution_subtract_fusion.5
  296.2 3.1 convolution_add_fusion
  308.5 24.8 %reduce-scatter.5.cloned.1.call-done = f32[201,32]{0,1:T(8,128)} async-done(((f32[201,256]{0,1:T(8,128)}), f32[201,32]{0,1:T(8,128)}) %reduce-scatter.5.cloned.1.call-update) | async-done | bytes 25744 | tf_op jit(solution)/shard_map/reduce_scatter | solution.py:93
  333.3 78.7 %reduce-scatter.7.cloned.1.call-done = f32[201,32]{0,1:T(8,128)} async-done(((f32[201,256]{0,1:T(8,128)}), f32[201,32]{0,1:T(8,128)}) %reduce-scatter.7.cloned.1.call-update) | async-done | bytes 25744 | tf_op jit(solution)/shard_map/reduce_scatter | solution.py:93
  412.1 78.2 %reduce-scatter.9.cloned.1.call-done = f32[201,32]{0,1:T(8,128)} async-done(((f32[201,256]{0,1:T(8,128)}), f32[201,32]{0,1:T(8,128)}) %reduce-scatter.9.cloned.1.call-update) | async-done | bytes 25744 | tf_op jit(solution)/shard_map/reduce_scatter | solution.py:93
  490.2 78.5 %reduce-scatter.11.cloned.1.call-done = f32[201,32]{0,1:T(8,128)} async-done(((f32[201,256]{0,1:T(8,128)}), f32[201,32]{0,1:T(8,128)}) %reduce-scatter.11.cloned.1.call-update) | async-done | bytes 25744 | tf_op jit(solution)/shard_map/reduce_scatter | solution.py:93
  (132 shorter events, 140.4 us)
Async XLA Ops:
  6.5 2.3 copy-start.15
  6.5 326.8 %reduce-scatter.5.cloned.1.call-start = ((), (), s32[]{:S(2)}) async-start(), calls=%async_computation.4 | async-start | bytes 294912 | tf_op jit(solution)/shard_map/reduce_scatter | solution.py:93
  8.0 1.2 copy-start
  9.7 43.3 %collective-permute-start.3 = (bf16[2,256,4,256]{3,2,1,0:T(4,128)(2,1)S(1)}, bf16[2,256,4,256]{3,2,1,0:T(4,128)(2,1)}, u32[]{:S(2)}, u32[]{:S(2)}) collective-permute-start(bf16[2,256,4,256]{3,2,1,0:T(4,128)(2,1)S(1)} %multiply_convert_fusion), channel_id=1, source_target_pairs={{0,32},{8,40},{16,48},{24,56},{32,64},{40,72},{48,80},{56,88},{64,... | collective-permute-start | bytes 3145736 | tf_op jit(solution)/shard_map/ppermute | solution.py:15
  16.4 75.1 %collective-permute-start.2 = (bf16[2,256,4,256]{3,2,1,0:T(4,128)(2,1)S(1)}, bf16[2,256,4,256]{3,2,1,0:T(4,128)(2,1)}, u32[]{:S(2)}, u32[]{:S(2)}) collective-permute-start(bf16[2,256,4,256]{3,2,1,0:T(4,128)(2,1)S(1)} %multiply_convert_fusion), channel_id=1, source_target_pairs={{0,24},{8,32},{16,40},{24,48},{32,56},{40,64},{48,72},{56,80},{64,... | collective-permute-start | bytes 3145736 | tf_op jit(solution)/shard_map/ppermute | solution.py:15
  23.5 92.5 %collective-permute-start.1 = (bf16[2,256,4,256]{3,2,1,0:T(4,128)(2,1)S(1)}, bf16[2,256,4,256]{3,2,1,0:T(4,128)(2,1)}, u32[]{:S(2)}, u32[]{:S(2)}) collective-permute-start(bf16[2,256,4,256]{3,2,1,0:T(4,128)(2,1)S(1)} %multiply_convert_fusion), channel_id=1, source_target_pairs={{0,16},{8,24},{16,32},{24,40},{32,48},{40,56},{48,64},{56,72},{64,... | collective-permute-start | bytes 3145736 | tf_op jit(solution)/shard_map/ppermute | solution.py:15
  26.1 102.3 %collective-permute-start = (bf16[2,256,4,256]{3,2,1,0:T(4,128)(2,1)S(1)}, bf16[2,256,4,256]{3,2,1,0:T(4,128)(2,1)}, u32[]{:S(2)}, u32[]{:S(2)}) collective-permute-start(bf16[2,256,4,256]{3,2,1,0:T(4,128)(2,1)S(1)} %multiply_convert_fusion), channel_id=1, source_target_pairs={{0,8},{8,16},{16,24},{24,32},{32,40},{40,48},{48,56},{56,64},{64,7... | collective-permute-start | bytes 3145736 | tf_op jit(solution)/shard_map/ppermute | solution.py:15
  28.4 5.6 copy-start.12
  34.2 6.9 %copy-start.10 = (bf16[32,8,4,256]{3,1,2,0:T(8,128)(2,1)}, bf16[32,8,4,256]{3,1,2,0:T(8,128)(2,1)S(1)}, u32[]{:S(2)}) copy-start(bf16[32,8,4,256]{3,1,2,0:T(8,128)(2,1)S(1)} %copy.3) | copy-start | bytes 1572868
  44.5 4.7 copy-start.4
  44.5 4.7 copy-start.11
  154.2 6.1 %copy-start.6 = (bf16[32,8,4,256]{3,1,2,0:T(8,128)(2,1)}, bf16[32,8,4,256]{3,1,2,0:T(8,128)(2,1)S(1)}, u32[]{:S(2)}) copy-start(bf16[32,8,4,256]{3,1,2,0:T(8,128)(2,1)S(1)} %copy.8) | copy-start | bytes 1572868
  164.9 5.7 copy-start.8
  179.9 3.9 copy-start.3
  179.9 3.9 copy-start.7
  183.9 2.4 copy-start.5
  183.9 2.4 copy-start.9
  194.5 3.5 copy-start.1
  194.5 3.5 copy-start.2
  197.9 3.5 copy-start.13
  255.9 156.2 %reduce-scatter.7.cloned.1.call-start = ((), (), s32[]{:S(2)}) async-start(), calls=%async_computation.5 | async-start | bytes 294912 | tf_op jit(solution)/shard_map/reduce_scatter | solution.py:93
  258.3 1.3 copy-start.18
  258.4 4.2 copy-start.17
  282.8 8.3 %copy-start.14 = (f32[512,256]{1,0:T(8,128)S(1)}, f32[512,256]{1,0:T(8,128)}, u32[]{:S(2)}) copy-start(f32[512,256]{1,0:T(8,128)} %reduce_sum.87) | copy-start | bytes 1572868
  282.8 8.3 %copy-start.16 = (f32[256,256]{1,0:T(8,128)S(1)}, f32[256,256]{1,0:T(8,128)}, u32[]{:S(2)}) copy-start(f32[256,256]{1,0:T(8,128)} %fusion.77) | copy-start | bytes 786436
  291.2 5.0 copy-start.19
  294.2 196.1 %reduce-scatter.9.cloned.1.call-start = ((), (), s32[]{:S(2)}) async-start(), calls=%async_computation.6 | async-start | bytes 294912 | tf_op jit(solution)/shard_map/reduce_scatter | solution.py:93
  305.2 263.5 %reduce-scatter.11.cloned.1.call-start = ((), (), s32[]{:S(2)}) async-start(), calls=%async_computation.7 | async-start | bytes 294912 | tf_op jit(solution)/shard_map/reduce_scatter | solution.py:93
Sparse Core Ops, SparseCore 0:
  256.0 77.2 reduce-scatter.4
  337.7 74.3 reduce-scatter.6
  415.9 74.2 reduce-scatter.8
  494.4 74.2 reduce-scatter.10
where the time goes:
time: 587 us; the launch traced here: 577 us
  waiting for transfers between devices  317 us (54%)
  matrix products  186 us (32%)
  local copies, waits for them, and re-layouts  26.3 us (4%)
  starting transfers between devices  18.4 us (3%)
  other arithmetic  15.2 us (3%)
  between operations  14 us (2%)
    reduce_scatter x4, waiting for transfers between devices, on_device(): lax.psum_scatter(partial_term, 'frq', scatter_dimension=1, tiled=True)  260 us
    dot_general x24, matrix products, matmul_high(): jnp.dot(left, right, precision=lax.Precision.HIGHEST, preferred_element_t...  66.3 us
    dot_general x20, matrix products, twiddle_product(): jnp.dot(pair[1], data, preferred_element_type=jnp.float32)  64.3 us
    ppermute x4, waiting for transfers between devices, from_behind(): lax.ppermute(value, axis, [(source, source + steps) for source in range(f...  56.5 us
    dot_general x20, matrix products, twiddle_product(): jnp.dot(pair[0], data, preferred_element_type=jnp.float32)  55.7 us
    ppermute x4, starting transfers between devices, from_behind(): lax.ppermute(value, axis, [(source, source + steps) for source in range(f...  18.2 us
  transfers between devices with their start and end apart: 8, of which 7 were waited for; matrix products, arithmetic and copies ran while one was open for 17% of the time, Pallas kernels for 0%

commit v1 on v0

v1 whole, which is shorter than its diff:
```python
import functools
import math

import jax
import jax.numpy as jnp
import ml_dtypes
import numpy as np
from jax import lax
from jax.experimental import pallas as pl
from jax.experimental.pallas import tpu as pltpu
from jax.sharding import PartitionSpec as P

LAGS = 201
ROUNDS = 4
CB = 256
W = 4
M = 384
K = 128
TAU = 256
MESH = pl.DeviceIdType.MESH
PAIRS = 8


def forward_table():
    angle = 2.0 * np.pi / M * (np.outer(np.arange(M), np.arange(CB)) % M)
    cos, sin = np.cos(angle), np.sin(angle)
    return np.block([[cos, sin], [-sin, cos]]).astype(ml_dtypes.bfloat16)


def inverse_table(scale):
    angle = 2.0 * np.pi / M * (np.outer(np.arange(CB) - CB // 2, np.arange(M)) % M)
    cos, sin = scale * np.cos(angle), scale * np.sin(angle)
    return np.block([[cos, -sin], [sin, cos]]).astype(ml_dtypes.bfloat16)


def lag_table(freq_total):
    lag = np.arange(TAU) - (LAGS - 1) // 2
    angle = np.pi / freq_total * (np.outer(np.arange(freq_total), lag) % (2 * freq_total))
    keep = np.arange(TAU) < LAGS
    cos = np.where(keep, np.cos(angle), 0.0).reshape(-1, K, TAU)
    sin = np.where(keep, np.sin(angle), 0.0).reshape(-1, K, TAU)
    return np.concatenate([cos, -sin], axis=1).astype(ml_dtypes.bfloat16)


PAIR_LIST = (
    ((0, 0), (1, 1)),
    ((0, 0), (1, 0)),
    ((2, 0), (1, 1)),
    ((2, 0), (1, 0)),
    ((0, 1), (0, 0)),
    ((0, 1), (1, 1)),
    ((0, 1), (1, 0)),
    ((2, 1), (1, 1)),
)


def kernel(
    n_blk, n_frq, x_ref, fwd_hbm, inv_hbm, lag_hbm, out_ref,
    fwd, inv, lag, near, hats, acc, part_out, part_in, piece_out, piece_in,
    table_sem, local_sem, send_sem, recv_sem, part_send, part_recv, piece_send, piece_recv,
):
    blk = lax.axis_index("blk")
    frq = lax.axis_index("frq")
    chips = n_blk // 2
    rows = CB // n_frq
    chip, core = blk // 2, blk % 2
    right = (chip + 1) % chips
    left = (chip + chips - 1) % chips

    barrier = pltpu.get_barrier_semaphore()
    peers = [(chip * 2 + 1 - core, frq)]
    for c in range(2):
        peers += [(right * 2 + c, frq), (left * 2 + c, frq)]
    for off in range(1, n_frq):
        other = (frq + off) % n_frq
        peers += [(blk, other), (right * 2 + core, other), (left * 2 + core, other)]
    for peer in peers:
        pl.semaphore_signal(barrier, inc=1, device_id=peer, device_id_type=MESH)

    tables = [
        pltpu.make_async_copy(fwd_hbm, fwd, table_sem.at[0]),
        pltpu.make_async_copy(inv_hbm, inv, table_sem.at[1]),
        pltpu.make_async_copy(lag_hbm.at[frq * 2 + core], lag, table_sem.at[2]),
    ]
    for copy in tables:
        copy.start()
    acc[...] = jnp.zeros_like(acc)
    pl.semaphore_wait(barrier, len(peers))

    def local_copy(w):
        return pltpu.make_async_copy(x_ref.at[core, w], near.at[0, w, core], local_sem.at[w])

    def partner_copy(w):
        return pltpu.make_async_remote_copy(
            src_ref=x_ref.at[1 - core, w],
            dst_ref=near.at[0, w, core],
            send_sem=send_sem.at[0, w, 0],
            recv_sem=recv_sem.at[0, w, core],
            device_id=(chip * 2 + 1 - core, frq),
            device_id_type=MESH,
        )

    def chip_copy(slot, w, half):
        return pltpu.make_async_remote_copy(
            src_ref=x_ref.at[half, w],
            dst_ref=near.at[slot, w, core],
            send_sem=send_sem.at[slot, w, half],
            recv_sem=recv_sem.at[slot, w, core],
            device_id=((right if slot == 1 else left) * 2 + half, frq),
            device_id_type=MESH,
        )

    for w in range(W):
        local_copy(w).start()
        for half in range(2):
            chip_copy(1, w, half).start()
            chip_copy(2, w, half).start()
        partner_copy(w).start()
    for copy in tables:
        copy.wait()

    def wait_landed(slot, w, c):
        pltpu.make_async_copy(near.at[slot, w, c], near.at[slot, w, c], recv_sem.at[slot, w, c]).wait()

    def hat(slot, w):
        data = jnp.concatenate([near[slot, w, 0], near[slot, w, 1]], axis=1)
        hats[slot] = jnp.dot(fwd[...], data, preferred_element_type=jnp.float32)

    def window(w, carry):
        local_copy(w).wait()
        wait_landed(0, w, 1 - core)
        hat(0, w)
        for slot in (1, 2):
            for c in range(2):
                wait_landed(slot, w, c)
            hat(slot, w)

        def tile(t, inner):
            re = pl.ds(pl.multiple_of(t * 8, 8), 8)
            im = pl.ds(pl.multiple_of(M + t * 8, 8), 8)
            value = {}
            for slot in range(3):
                for c in range(2):
                    lanes = slice(c * K, (c + 1) * K)
                    value[slot, c] = (hats[slot, re, lanes], hats[slot, im, lanes])
            for index, (one, two) in enumerate(PAIR_LIST):
                (ar, ai), (br, bi) = value[one], value[two]
                acc[index, re] += ar * br + ai * bi
                acc[index, im] += ai * br - ar * bi
            return inner

        return lax.fori_loop(0, M // 8, tile, carry)

    lax.fori_loop(0, W, window, 0)

    def correlations(index):
        both = jnp.concatenate([acc[index], acc[index + 1]], axis=1).astype(jnp.bfloat16)
        stack = jnp.dot(inv[...], both, preferred_element_type=jnp.float32).astype(jnp.bfloat16)
        for c in range(2):
            lanes = slice(c * K, (c + 1) * K)
            pair = jnp.concatenate([stack[:CB, lanes], stack[CB:, lanes]], axis=1)
            yield jnp.dot(pair, lag[...], preferred_element_type=jnp.float32)

    def part_copy(j):
        return pltpu.make_async_remote_copy(
            src_ref=part_out.at[j],
            dst_ref=part_in.at[j],
            send_sem=part_send.at[j],
            recv_sem=part_recv.at[j],
            device_id=(chip * 2 + 1 - core, frq),
            device_id_type=MESH,
        )

    for j in range(0, ROUNDS, 2):
        for c, value in enumerate(correlations((1 - core) * ROUNDS + j)):
            part_out[j + c] = value.astype(jnp.bfloat16)
            part_copy(j + c).start()

    def owner(j):
        shift = (0, 0, 1 - core, 1)[j]
        return ((chip + shift) % chips) * 2 + core

    def piece_copy(j, off):
        other = (frq + off) % n_frq
        return pltpu.make_async_remote_copy(
            src_ref=piece_out.at[j, pl.ds(pl.multiple_of(other * rows, rows), rows)],
            dst_ref=piece_in.at[j, frq],
            send_sem=piece_send.at[j, off],
            recv_sem=piece_recv.at[j, frq],
            device_id=(owner(j), other),
            device_id_type=MESH,
        )

    def own_copy(j):
        return pltpu.make_async_copy(
            piece_out.at[j, pl.ds(pl.multiple_of(frq * rows, rows), rows)],
            piece_in.at[j, frq],
            piece_recv.at[j, frq],
        )

    for j in range(0, ROUNDS, 2):
        for c, value in enumerate(correlations(core * ROUNDS + j)):
            part_copy(j + c).wait_recv()
            piece_out[j + c] = (value + part_in[j + c].astype(jnp.float32)).astype(jnp.bfloat16)
            for off in range(1, n_frq):
                piece_copy(j + c, off).start()
            if j + c < 2:
                own_copy(j + c).start()
            elif j + c == 3:
                piece_copy(j + c, 0).start()
            else:
                @pl.when(core == 0)
                def _():
                    piece_copy(2, 0).start()

                @pl.when(core == 1)
                def _():
                    own_copy(2).start()

    for j in range(ROUNDS):
        total = jnp.zeros((rows, TAU), jnp.float32)
        for f in range(n_frq):
            pltpu.make_async_copy(piece_in.at[j, f], piece_in.at[j, f], piece_recv.at[j, f]).wait()
            total += piece_in[j, f].astype(jnp.float32)
        total = jnp.where(blk > j, total, 0.0)
        out_ref[j] = total[:, :LAGS]

    for w in range(W):
        partner_copy(w).wait_send()
        for half in range(2):
            chip_copy(1, w, half).wait_send()
            chip_copy(2, w, half).wait_send()
    for j in range(ROUNDS):
        part_copy(j).wait_send()
        for off in range(1, n_frq):
            piece_copy(j, off).wait_send()
    piece_copy(3, 0).wait_send()

    @pl.when(core == 0)
    def _():
        piece_copy(2, 0).wait_send()


def on_device(n_blk, n_frq, spectra, channel_valid):
    freq_local = spectra.shape[3]
    freq_total = freq_local * n_frq
    spectra_f = spectra.astype(jnp.float32)
    mean_power = jnp.mean(
        spectra_f[0] * spectra_f[0] + spectra_f[1] * spectra_f[1], axis=1, keepdims=True
    )
    whiten_scale = channel_valid.astype(jnp.float32)[:, None, None] / jnp.maximum(
        jnp.sqrt(mean_power), 0.5
    )
    whitened = (spectra_f * whiten_scale[None]).astype(jnp.bfloat16)
    halves = whitened.reshape(2, CB, W, 2, K).transpose(3, 2, 0, 1, 4).reshape(2, W, 2 * CB, K)
    rows = CB // n_frq
    scale = 1.0 / (M * math.sqrt(W * CB * freq_total))
    vmem = pl.BlockSpec(memory_space=pltpu.VMEM)
    hbm = pl.BlockSpec(memory_space=pl.ANY)
    dma = pltpu.SemaphoreType.DMA
    stacked = pl.pallas_call(
        functools.partial(kernel, n_blk, n_frq),
        out_shape=jax.ShapeDtypeStruct((ROUNDS, rows, LAGS), jnp.float32),
        in_specs=[vmem, hbm, hbm, hbm],
        out_specs=vmem,
        scratch_shapes=[
            pltpu.VMEM((2 * M, 2 * CB), jnp.bfloat16),
            pltpu.VMEM((2 * CB, 2 * M), jnp.bfloat16),
            pltpu.VMEM((2 * K, TAU), jnp.bfloat16),
            pltpu.VMEM((3, W, 2, 2 * CB, K), jnp.bfloat16),
            pltpu.VMEM((3, 2 * M, 2 * K), jnp.float32),
            pltpu.VMEM((PAIRS, 2 * M, K), jnp.float32),
            pltpu.VMEM((ROUNDS, CB, TAU), jnp.bfloat16),
            pltpu.VMEM((ROUNDS, CB, TAU), jnp.bfloat16),
            pltpu.VMEM((ROUNDS, CB, TAU), jnp.bfloat16),
            pltpu.VMEM((ROUNDS, n_frq, rows, TAU), jnp.bfloat16),
            dma((3,)),
            dma((W,)),
            dma((3, W, 2)),
            dma((3, W, 2)),
            dma((ROUNDS,)),
            dma((ROUNDS,)),
            dma((ROUNDS, n_frq)),
            dma((ROUNDS, n_frq)),
        ],
        compiler_params=pltpu.CompilerParams(collective_id=0, has_side_effects=True),
    )(
        halves,
        jnp.asarray(forward_table()),
        jnp.asarray(inverse_table(scale)),
        jnp.asarray(lag_table(freq_total)),
    )
    return stacked.transpose(0, 2, 1)[None]


def solution(mesh):
    return jax.shard_map(
        functools.partial(on_device, mesh.shape["blk"], mesh.shape["frq"]),
        mesh=mesh,
        in_specs=(P(None, "blk", None, "frq"), P("blk")),
        out_specs=P("blk", None, None, "frq"),
        check_vma=False,
    )
```

time: 587 us -> 58.2 us (0.10); the launches traced: 577 us -> 58 us
  waiting for transfers between devices: 317 us -> 0 us
  matrix products: 186 us -> 0 us
  Pallas kernels: 0 us -> 51.6 us
  local copies, waits for them, and re-layouts: 26.3 us -> 3.51 us
  starting transfers between devices: 18.4 us -> 0 us
  between operations: 14 us -> 0.06 us
  other arithmetic: 15.2 us -> 2.86 us
    reduce_scatter x4 -> x0, waiting for transfers between devices: 260 us -> none  [on_device(): lax.psum_scatter(partial_term, 'frq', scatter_dimension=1, tiled=True)]
    dot_general x64 -> x0, matrix products: 186 us -> none  [the longest x24 66.3 us: matmul_high(): jnp.dot(left, right, precision=lax.Precision.HIGHEST, preferred_element_t...]
    ppermute x4 -> x0, waiting for transfers between devices: 56.5 us -> none  [from_behind(): lax.ppermute(value, axis, [(source, source + steps) for source in range(f...]
    pallas_call x0 -> x1, Pallas kernels: none -> 51.6 us  [on_device(): pl.pallas_call(functools.partial(kernel, n_blk, n_frq), out_shape=jax.Sha...]
    ppermute x4 -> x0, starting transfers between devices: 18.2 us -> none  [from_behind(): lax.ppermute(value, axis, [(source, source + steps) for source in range(f...]
    reduce_sum x8 -> x0, other arithmetic: 10.8 us -> none  [the longest x4 5.86 us: lag_terms(): jnp.sum(own_hat[1] * far_hat[0] - own_hat[0] * far_hat[1], axis=1)]
    sub x4 -> x0, local copies, waits for them, and re-layouts: 9.42 us -> none  [lag_terms(): own_hat[1] * far_hat[0] - own_hat[0] * far_hat[1]]
    add x4 -> x0, local copies, waits for them, and re-layouts: 8.96 us -> none  [lag_terms(): own_hat[0] * far_hat[0] + own_hat[1] * far_hat[1]]
  transfers between devices with their start and end apart: 8 -> 0, of which waited for: 7 -> 0; matrix products, arithmetic and copies ran while one was open for 17% -> 0% of each run, Pallas kernels for 0% -> 0%
where the time goes in v1:
time: 58.2 us; the launch traced here: 58 us
  Pallas kernels  51.6 us (89%)
  local copies, waits for them, and re-layouts  3.51 us (6%)
  other arithmetic  2.86 us (5%)
    pallas_call x1, Pallas kernels, on_device(): pl.pallas_call(functools.partial(kernel, n_blk, n_frq), out_shape=jax.Sha...  51.6 us
    unnamed x5, local copies, waits for them, and re-layouts  1.86 us
    reshape x2, local copies, waits for them, and re-layouts, on_device(): whitened.reshape(2, CB, W, 2, K).transpose(3, 2, 0, 1, 4)  1.65 us
    convert_element_type x1, other arithmetic, on_device(): spectra_f = spectra.astype(jnp.float32)  1.51 us

profile of v1, /device:TPU:1, one launch (start us, length us, event | category | flops | bytes accessed | tf_op | source)
XLA Modules:
  0.0 58.0 jit_solution(10701445474650177992)
XLA Ops:
  0.0 0.0 copy-start.1
  0.0 1.5 %convert_element_type.9 = f32[2,256,4,256]{3,2,1,0:T(4,128)S(1)} convert(bf16[2,256,4,256]{3,2,1,0:T(4,128)(2,1)} %param.5) | non-fusion elementwise | flops 524288 | bytes 3145728 | tf_op jit(solution)/shard_map/convert_element_type | solution.py:247
  1.5 0.0 copy-start
  1.5 0.8 %fusion.1 = f32[256,256]{1,0:T(8,128)S(1)} fusion(f32[2,256,4,256]{3,2,1,0:T(4,128)S(1)} %convert_element_type.9), kind=kLoop, calls=%fused_computation.3 | loop fusion | flops 983040 | bytes 2359296 | tf_op jit(solution)/shard_map/reduce_sum | solution.py:248
  2.3 0.0 copy-done.1
  2.3 0.1 maximum_divide_fusion
  2.5 0.3 copy-done
  2.7 0.5 multiply_convert_fusion
  3.2 0.4 reshape.34
  3.6 1.2 %copy.6 = bf16[2,256,4,2,128]{4,1,0,2,3:T(8,128)(2,1)} copy(bf16[2,256,4,2,128]{4,3,2,1,0:T(2,128)(2,1)S(1)} %reshape.34) | data formatting | bytes 2097152 | tf_op jit(solution)/shard_map/reshape | solution.py:255
  4.9 51.6 %shard_map.55 = f32[4,32,201]{2,1,0:T(8,128)} custom-call(bf16[2,4,512,128]{3,2,1,0:T(8,128)(2,1)} %bitcast.6, bf16[768,512]{1,0:T(8,128)(2,1)} %constant.13.clone.fwd_hbm, bf16[512,768]{1,0:T(8,128)(2,1)} %constant.14.clone.inv_hbm, bf16[16,256,256]{2,1,0:T(8,128)(2,1)} %constant.15.clone.lag_hbm), custom_call_target="tpu_custom_call" | custom-call | tf_op jit(solution)/shard_map/pallas_call | solution.py:261
  56.4 1.6 %copy.8 = f32[1,4,201,32]{2,3,1,0:T(8,128)} copy(f32[1,4,201,32]{2,3,1,0:T(8,128)} %bitcast.7) | data formatting | bytes 205824
  (1 shorter events, 0.0 us)
Async XLA Ops:
  0.0 2.3 %copy-start.1 = (s32[256]{0:T(256)S(1)}, s32[256]{0:T(256)}, u32[]{:S(2)}) copy-start(s32[256]{0:T(256)} %param.6) | copy-start | bytes 3076
  1.5 1.2 %copy-start = (bf16[2,256,4,256]{3,2,1,0:T(4,128)(2,1)S(1)}, bf16[2,256,4,256]{3,2,1,0:T(4,128)(2,1)}, u32[]{:S(2)}) copy-start(bf16[2,256,4,256]{3,2,1,0:T(4,128)(2,1)} %param.5) | copy-start | bytes 3145732

commit v2 on v1

v2 whole, which is shorter than its diff:
```python
import functools
import math

import jax
import jax.numpy as jnp
import ml_dtypes
import numpy as np
from jax import lax
from jax.experimental import pallas as pl
from jax.experimental.pallas import tpu as pltpu
from jax.sharding import PartitionSpec as P

LAGS = 201
ROUNDS = 4
CB = 256
W = 4
M = 384
K = 128
TAU = 256
EARLY = 3
MESH = pl.DeviceIdType.MESH


def forward_table():
    angle = 2.0 * np.pi / M * (np.outer(np.arange(M), np.arange(CB)) % M)
    cos, sin = np.cos(angle), np.sin(angle)
    return np.block([[cos, sin], [-sin, cos]]).astype(ml_dtypes.bfloat16)


def inverse_table(scale):
    angle = 2.0 * np.pi / M * (np.outer(np.arange(CB) - CB // 2, np.arange(M)) % M)
    cos, sin = scale * np.cos(angle), scale * np.sin(angle)
    return np.block([[cos, -sin], [sin, cos]]).astype(ml_dtypes.bfloat16)


def lag_tables(freq_total):
    lag = np.arange(TAU) - (LAGS - 1) // 2
    keep = np.arange(TAU) < LAGS

    def waves(freq):
        angle = np.pi / freq_total * (np.outer(freq, lag) % (2 * freq_total))
        return np.stack([np.where(keep, np.cos(angle), 0.0), np.where(keep, np.sin(angle), 0.0)])

    fine = waves(np.arange(K)).astype(np.float32)
    coarse = waves(np.arange(0, freq_total, K)).transpose(1, 0, 2).astype(np.float32)
    return fine, coarse


C, D, B, E, A, F = (0, 0), (0, 1), (1, 0), (1, 1), (2, 0), (2, 1)
PHASE_PAIRS = (
    ((C, B), (E, B), (D, C), (D, B)),
    ((C, A), (E, A), (D, A), (F, B)),
)


def kernel(
    n_blk, n_frq, raw_hbm, valid_ref, fwd_hbm, inv_hbm, fine_hbm, coarse_hbm, out_ref,
    raw, fwd, inv, fine, coarse, lag, column, mine, near, hats, acc, part_out, part_in, piece_out, piece_in,
    load_sem, local_sem, send_sem, recv_sem, part_send, part_recv, piece_send, piece_recv,
):
    blk = lax.axis_index("blk")
    frq = lax.axis_index("frq")
    chips = n_blk // 2
    rows = CB // n_frq
    chip, core = blk // 2, blk % 2
    right = (chip + 1) % chips
    left = (chip + chips - 1) % chips
    partner = (chip * 2 + 1 - core, frq)

    loads = [
        pltpu.make_async_copy(raw_hbm, raw, load_sem.at[0]),
        pltpu.make_async_copy(fwd_hbm, fwd, load_sem.at[1]),
        pltpu.make_async_copy(inv_hbm, inv, load_sem.at[2]),
        pltpu.make_async_copy(fine_hbm, fine, load_sem.at[3]),
        pltpu.make_async_copy(coarse_hbm.at[frq * 2 + core], coarse, load_sem.at[4]),
    ]
    for copy in loads:
        copy.start()

    barrier = pltpu.get_barrier_semaphore()
    peers = [partner]
    for c in range(2):
        peers += [(right * 2 + c, frq), (left * 2 + c, frq)]
    for off in range(1, n_frq):
        other = (frq + off) % n_frq
        peers += [(blk, other), (right * 2 + core, other), (left * 2 + core, other)]
    for peer in peers:
        pl.semaphore_signal(barrier, inc=1, device_id=peer, device_id_type=MESH)

    here = lax.broadcasted_iota(jnp.int32, (K, K), 0) == lax.broadcasted_iota(jnp.int32, (K, K), 1)
    for part in range(CB // K):
        row = valid_ref[part : part + 1, :].astype(jnp.float32)
        spread = jnp.where(here, jnp.broadcast_to(row, (K, K)), 0.0)
        total = jnp.sum(spread, axis=1, keepdims=True)
        column[part * K : (part + 1) * K] = jnp.broadcast_to(total, (K, K))

    loads[0].wait()

    def whiten(t, carry):
        real = pl.ds(pl.multiple_of(t * 16, 16), 16)
        imag = pl.ds(pl.multiple_of(CB + t * 16, 16), 16)
        keep = column[real]
        for half in range(2):
            values = [
                (raw[half, w, real].astype(jnp.float32), raw[half, w, imag].astype(jnp.float32))
                for w in range(W)
            ]
            power = sum(re * re + im * im for re, im in values) * (1.0 / W)
            factor = keep / jnp.maximum(jnp.sqrt(power), 0.5)
            for w, (re, im) in enumerate(values):
                mine[half, w, real] = (re * factor).astype(jnp.bfloat16)
                mine[half, w, imag] = (im * factor).astype(jnp.bfloat16)
        return carry

    lax.fori_loop(0, CB // 16, whiten, 0, unroll=2)
    pl.semaphore_wait(barrier, len(peers))

    def local_copy(w):
        return pltpu.make_async_copy(mine.at[core, w], near.at[0, w, core], local_sem.at[w])

    def partner_copy(w):
        return pltpu.make_async_remote_copy(
            src_ref=mine.at[1 - core, w],
            dst_ref=near.at[0, w, core],
            send_sem=send_sem.at[0, w, 0],
            recv_sem=recv_sem.at[0, w, core],
            device_id=partner,
            device_id_type=MESH,
        )

    def chip_copy(phase, w, half):
        rightward = core == (1 if phase == 1 else 0)
        side = 1 - core if phase == 1 else core
        return pltpu.make_async_remote_copy(
            src_ref=mine.at[half, w],
            dst_ref=near.at[phase, w, side],
            send_sem=send_sem.at[phase, w, half],
            recv_sem=recv_sem.at[phase, w, side],
            device_id=(jnp.where(rightward, right, left) * 2 + half, frq),
            device_id_type=MESH,
        )

    for w in range(W):
        for half in range(2):
            chip_copy(1, w, half).start()
        partner_copy(w).start()
        local_copy(w).start()

    acc[...] = jnp.zeros_like(acc)
    for copy in loads[1:]:
        copy.wait()
    fine_cos, fine_sin = fine[0], fine[1]
    coarse_cos, coarse_sin = coarse[0:1], coarse[1:2]
    lag[:K] = (fine_cos * coarse_cos - fine_sin * coarse_sin).astype(jnp.bfloat16)
    lag[K:] = (-(fine_sin * coarse_cos + fine_cos * coarse_sin)).astype(jnp.bfloat16)

    def wait_landed(slot, w, c):
        pltpu.make_async_copy(near.at[slot, w, c], near.at[slot, w, c], recv_sem.at[slot, w, c]).wait()

    def hat(slot, w):
        data = jnp.concatenate([near[slot, w, 0], near[slot, w, 1]], axis=1)
        hats[slot, w] = jnp.dot(fwd[...], data, preferred_element_type=jnp.float32)

    def cross(phase, w):
        pairs = PHASE_PAIRS[phase - 1]
        used = sorted({block for pair in pairs for block in pair})

        def tile(t, carry):
            re = pl.ds(pl.multiple_of(t * 8, 8), 8)
            im = pl.ds(pl.multiple_of(M + t * 8, 8), 8)
            value = {}
            for slot, c in used:
                lanes = slice(c * K, (c + 1) * K)
                value[slot, c] = (hats[slot, w, re, lanes], hats[slot, w, im, lanes])
            for index, (one, two) in enumerate(pairs):
                (ar, ai), (br, bi) = value[one], value[two]
                acc[phase - 1, index, re] += ar * br + ai * bi
                acc[phase - 1, index, im] += ai * br - ar * bi
            return carry

        lax.fori_loop(0, M // 8, tile, 0, unroll=2)

    def correlations(phase, index):
        both = jnp.concatenate([acc[phase - 1, index], acc[phase - 1, index + 1]], axis=1)
        stack = jnp.dot(inv[...], both.astype(jnp.bfloat16), preferred_element_type=jnp.float32)
        stack = stack.astype(jnp.bfloat16)
        for c in range(2):
            lanes = slice(c * K, (c + 1) * K)
            pair = jnp.concatenate([stack[:CB, lanes], stack[CB:, lanes]], axis=1)
            yield jnp.dot(pair, lag[...], preferred_element_type=jnp.float32)

    def part_copy(phase, i):
        return pltpu.make_async_remote_copy(
            src_ref=part_out.at[phase - 1, i],
            dst_ref=part_in.at[phase - 1, i],
            send_sem=part_send.at[phase - 1, i],
            recv_sem=part_recv.at[phase - 1, i],
            device_id=partner,
            device_id_type=MESH,
        )

    def place(phase, i):
        if phase == 1:
            return (0, 0) if i == 0 else (2 - core, 1 - core)
        return (1 + core, 0) if i == 0 else (3, 1)

    def piece_rows(other):
        return pl.ds(pl.multiple_of(other * rows, rows), rows)

    def piece_copy(phase, i, off):
        j, shift = place(phase, i)
        other = (frq + off) % n_frq
        return pltpu.make_async_remote_copy(
            src_ref=piece_out.at[phase - 1, i, piece_rows(other)],
            dst_ref=piece_in.at[j, frq],
            send_sem=piece_send.at[phase - 1, i, off],
            recv_sem=piece_recv.at[j, frq],
            device_id=((chip + shift) % chips * 2 + core, other),
            device_id_type=MESH,
        )

    def own_copy(phase, i):
        j, _ = place(phase, i)
        return pltpu.make_async_copy(
            piece_out.at[phase - 1, i, piece_rows(frq)], piece_in.at[j, frq], piece_recv.at[j, frq]
        )

    def scatter(phase):
        for i, value in enumerate(correlations(phase, (1 - core) * 2)):
            part_out[phase - 1, i] = value.astype(jnp.bfloat16)
            part_copy(phase, i).start()
        for i, value in enumerate(correlations(phase, core * 2)):
            part_copy(phase, i).wait_recv()
            both = value + part_in[phase - 1, i].astype(jnp.float32)
            piece_out[phase - 1, i] = both.astype(jnp.bfloat16)
            for off in range(1, n_frq):
                piece_copy(phase, i, off).start()
            if i == 0:
                own_copy(phase, i).start()
            elif phase == 2:
                piece_copy(phase, i, 0).start()
            else:
                @pl.when(core == 0)
                def _():
                    piece_copy(1, 1, 0).start()

                @pl.when(core == 1)
                def _():
                    own_copy(1, 1).start()

    def first(w, carry):
        local_copy(w).wait()
        wait_landed(0, w, 1 - core)
        hat(0, w)
        for c in range(2):
            wait_landed(1, w, c)
        hat(1, w)
        cross(1, w)
        return carry

    lax.fori_loop(0, EARLY, first, 0)
    for w in range(W):
        for half in range(2):
            chip_copy(2, w, half).start()
    lax.fori_loop(EARLY, W, first, 0)
    scatter(1)

    def second(w, carry):
        for c in range(2):
            wait_landed(2, w, c)
        hat(2, w)
        cross(2, w)
        return carry

    lax.fori_loop(0, W, second, 0)
    scatter(2)

    for j in range(ROUNDS):
        total = jnp.zeros((rows, TAU), jnp.float32)
        for f in range(n_frq):
            pltpu.make_async_copy(piece_in.at[j, f], piece_in.at[j, f], piece_recv.at[j, f]).wait()
            total += piece_in[j, f].astype(jnp.float32)
        total = jnp.where(blk > j, total, 0.0)
        out_ref[j] = total[:, :LAGS]

    for w in range(W):
        partner_copy(w).wait_send()
        for half in range(2):
            chip_copy(1, w, half).wait_send()
            chip_copy(2, w, half).wait_send()
    for phase in (1, 2):
        for i in range(2):
            part_copy(phase, i).wait_send()
            for off in range(1, n_frq):
                piece_copy(phase, i, off).wait_send()
    piece_copy(2, 1, 0).wait_send()

    @pl.when(core == 0)
    def _():
        piece_copy(1, 1, 0).wait_send()


def on_device(n_blk, n_frq, spectra, channel_valid):
    freq_total = spectra.shape[3] * n_frq
    halves = spectra.reshape(2, CB, W, 2, K).transpose(3, 2, 0, 1, 4).reshape(2, W, 2 * CB, K)
    rows = CB // n_frq
    scale = 1.0 / (M * math.sqrt(W * CB * freq_total))
    vmem = pl.BlockSpec(memory_space=pltpu.VMEM)
    hbm = pl.BlockSpec(memory_space=pl.ANY)
    dma = pltpu.SemaphoreType.DMA
    fine, coarse = lag_tables(freq_total)
    stacked = pl.pallas_call(
        functools.partial(kernel, n_blk, n_frq),
        out_shape=jax.ShapeDtypeStruct((ROUNDS, rows, LAGS), jnp.float32),
        in_specs=[hbm, vmem, hbm, hbm, hbm, hbm],
        out_specs=vmem,
        scratch_shapes=[
            pltpu.VMEM((2, W, 2 * CB, K), jnp.bfloat16),
            pltpu.VMEM((2 * M, 2 * CB), jnp.bfloat16),
            pltpu.VMEM((2 * CB, 2 * M), jnp.bfloat16),
            pltpu.VMEM((2, K, TAU), jnp.float32),
            pltpu.VMEM((2, TAU), jnp.float32),
            pltpu.VMEM((2 * K, TAU), jnp.bfloat16),
            pltpu.VMEM((CB, K), jnp.float32),
            pltpu.VMEM((2, W, 2 * CB, K), jnp.bfloat16),
            pltpu.VMEM((3, W, 2, 2 * CB, K), jnp.bfloat16),
            pltpu.VMEM((3, W, 2 * M, 2 * K), jnp.float32),
            pltpu.VMEM((2, ROUNDS, 2 * M, K), jnp.float32),
            pltpu.VMEM((2, 2, CB, TAU), jnp.bfloat16),
            pltpu.VMEM((2, 2, CB, TAU), jnp.bfloat16),
            pltpu.VMEM((2, 2, CB, TAU), jnp.bfloat16),
            pltpu.VMEM((ROUNDS, n_frq, rows, TAU), jnp.bfloat16),
            dma((5,)),
            dma((W,)),
            dma((3, W, 2)),
            dma((3, W, 2)),
            dma((2, 2)),
            dma((2, 2)),
            dma((2, 2, n_frq)),
            dma((ROUNDS, n_frq)),
        ],
        compiler_params=pltpu.CompilerParams(collective_id=0, has_side_effects=True),
    )(
        halves,
        channel_valid.reshape(2, K),
        jnp.asarray(forward_table()),
        jnp.asarray(inverse_table(scale)),
        jnp.asarray(fine),
        jnp.asarray(coarse),
    )
    return stacked.transpose(0, 2, 1)[None]


def solution(mesh):
    return jax.shard_map(
        functools.partial(on_device, mesh.shape["blk"], mesh.shape["frq"]),
        mesh=mesh,
        in_specs=(P(None, "blk", None, "frq"), P("blk")),
        out_specs=P("blk", None, None, "frq"),
        check_vma=False,
    )
```

time: 58.2 us -> 55 us (0.945)
  other arithmetic: 2.86 us -> 0 us
  Pallas kernels: 51.6 us -> 50.5 us
  local copies, waits for them, and re-layouts: 3.51 us -> 4.24 us
    convert_element_type x3 -> x0, other arithmetic: 1.96 us -> none  [the longest x1 1.51 us: on_device(): spectra_f = spectra.astype(jnp.float32)]
    pallas_call x1, Pallas kernels: 51.6 us -> 50.5 us  [on_device(): pl.pallas_call(functools.partial(kernel, n_blk, n_frq), out_shape=jax.Sha...]
    reshape x2, local copies, waits for them, and re-layouts: 1.65 us -> 2.67 us  [on_device(): spectra.reshape(2, CB, W, 2, K).transpose(3, 2, 0, 1, 4)]
    reduce_sum x1 -> x0, other arithmetic: 0.78 us -> none  [on_device(): jnp.mean(spectra_f[0] * spectra_f[0] + spectra_f[1] * spectra_f[1], axis=...]
    unnamed x5 -> x1, local copies, waits for them, and re-layouts: 1.86 us -> 1.57 us
where the time goes in v2:
time: 55 us; the launch traced here: 54.8 us
  Pallas kernels  50.5 us (92%)
  local copies, waits for them, and re-layouts  4.24 us (8%)
    pallas_call x1, Pallas kernels, on_device(): pl.pallas_call(functools.partial(kernel, n_blk, n_frq), out_shape=jax.Sha...  50.5 us
    reshape x2, local copies, waits for them, and re-layouts, on_device(): spectra.reshape(2, CB, W, 2, K).transpose(3, 2, 0, 1, 4)  2.67 us
    unnamed x1, local copies, waits for them, and re-layouts  1.57 us

profile of v2, /device:TPU:1, one launch (start us, length us, event | category | flops | bytes accessed | tf_op | source)
XLA Modules:
  0.0 54.8 jit_solution(14214530718511301852)
XLA Ops:
  0.0 1.5 %reshape.9 = bf16[2,256,4,2,128]{4,3,2,1,0:T(2,128)(2,1)S(1)} reshape(bf16[2,256,4,256]{3,2,1,0:T(4,128)(2,1)} %param.6) | data formatting | bytes 2097152 | tf_op jit(solution)/shard_map/reshape | solution.py:305
  1.5 1.2 %copy.7 = bf16[2,256,4,2,128]{4,1,0,2,3:T(8,128)(2,1)} copy(bf16[2,256,4,2,128]{4,3,2,1,0:T(2,128)(2,1)S(1)} %reshape.9) | data formatting | bytes 2097152 | tf_op jit(solution)/shard_map/reshape | solution.py:305
  2.7 50.5 %shard_map.64 = f32[4,32,201]{2,1,0:T(8,128)} custom-call(bf16[2,4,512,128]{3,2,1,0:T(8,128)(2,1)} %bitcast.7, s32[2,128]{1,0:T(2,128)} %bitcast.9, bf16[768,512]{1,0:T(8,128)(2,1)} %constant.8.clone.fwd_hbm, bf16[512,768]{1,0:T(8,128)(2,1)} %constant.9.clone.inv_hbm, f32[2,128,256]{2,1,0:T(8,128)} %constant.10.clone.fine_hbm, ...), custom_call_target="tpu_custom_call" | custom-call | tf_op jit(solution)/shard_map/pallas_call | solution.py:312
  53.2 1.6 %copy.9 = f32[1,4,201,32]{2,3,1,0:T(8,128)} copy(f32[1,4,201,32]{2,3,1,0:T(8,128)} %bitcast.8) | data formatting | bytes 205824

commit v3 on v2

--- a/solution.py
+++ b/solution.py
@@ -56,7 +56,7 @@
 def kernel(
     n_blk, n_frq, raw_hbm, valid_ref, fwd_hbm, inv_hbm, fine_hbm, coarse_hbm, out_ref,
     raw, fwd, inv, fine, coarse, lag, column, mine, near, hats, acc, part_out, part_in, piece_out, piece_in,
-    load_sem, local_sem, send_sem, recv_sem, part_send, part_recv, piece_send, piece_recv,
+    load_sem, local_sem, send_sem, recv_sem, part_send, part_recv, piece_send, piece_recv, ready,
 ):
     blk = lax.axis_index("blk")
     frq = lax.axis_index("frq")
@@ -78,12 +78,12 @@
         copy.start()
 
     barrier = pltpu.get_barrier_semaphore()
-    peers = [partner]
+    side = n_frq // 2
+    next_x, last_x = frq // side * side + (frq + 1) % side, frq // side * side + (frq + side - 1) % side
+    across = (frq + side) % n_frq
+    peers = [partner, (blk, next_x), (blk, last_x), (blk, across)]
     for c in range(2):
         peers += [(right * 2 + c, frq), (left * 2 + c, frq)]
-    for off in range(1, n_frq):
-        other = (frq + off) % n_frq
-        peers += [(blk, other), (right * 2 + core, other), (left * 2 + core, other)]
     for peer in peers:
         pl.semaphore_signal(barrier, inc=1, device_id=peer, device_id_type=MESH)
 
@@ -101,10 +101,9 @@
         imag = pl.ds(pl.multiple_of(CB + t * 16, 16), 16)
         keep = column[real]
         for half in range(2):
-            values = [
-                (raw[half, w, real].astype(jnp.float32), raw[half, w, imag].astype(jnp.float32))
-                for w in range(W)
-            ]
+            lanes = slice(half * K, (half + 1) * K)
+            both = [jnp.swapaxes(raw[r, real, :, lanes].astype(jnp.float32), 0, 1) for r in range(2)]
+            values = [(both[0][w], both[1][w]) for w in range(W)]
             power = sum(re * re + im * im for re, im in values) * (1.0 / W)
             factor = keep / jnp.maximum(jnp.sqrt(power), 0.5)
             for w, (re, im) in enumerate(values):
@@ -145,6 +144,10 @@
             chip_copy(1, w, half).start()
         partner_copy(w).start()
         local_copy(w).start()
+
+    for step, target in enumerate([(blk, last_x), (blk, across), (left * 2 + core, frq)]):
+        pl.semaphore_signal(ready.at[step], inc=1, device_id=target, device_id_type=MESH)
+        pl.semaphore_wait(ready.at[step], 1)
 
     acc[...] = jnp.zeros_like(acc)
     for copy in loads[1:]:
@@ -302,7 +305,6 @@
 
 def on_device(n_blk, n_frq, spectra, channel_valid):
     freq_total = spectra.shape[3] * n_frq
-    halves = spectra.reshape(2, CB, W, 2, K).transpose(3, 2, 0, 1, 4).reshape(2, W, 2 * CB, K)
     rows = CB // n_frq
     scale = 1.0 / (M * math.sqrt(W * CB * freq_total))
     vmem = pl.BlockSpec(memory_space=pltpu.VMEM)
@@ -311,11 +313,11 @@
     fine, coarse = lag_tables(freq_total)
     stacked = pl.pallas_call(
         functools.partial(kernel, n_blk, n_frq),
-        out_shape=jax.ShapeDtypeStruct((ROUNDS, rows, LAGS), jnp.float32),
+        out_shape=pltpu.VMEM((ROUNDS, rows, LAGS), jnp.float32),
         in_specs=[hbm, vmem, hbm, hbm, hbm, hbm],
         out_specs=vmem,
         scratch_shapes=[
-            pltpu.VMEM((2, W, 2 * CB, K), jnp.bfloat16),
+            pltpu.VMEM((2, CB, W, 2 * K), jnp.bfloat16),
             pltpu.VMEM((2 * M, 2 * CB), jnp.bfloat16),
             pltpu.VMEM((2 * CB, 2 * M), jnp.bfloat16),
             pltpu.VMEM((2, K, TAU), jnp.float32),
@@ -338,10 +340,11 @@
             dma((2, 2)),
             dma((2, 2, n_frq)),
             dma((ROUNDS, n_frq)),
+            pltpu.SemaphoreType.REGULAR((3,)),
         ],
         compiler_params=pltpu.CompilerParams(collective_id=0, has_side_effects=True),
     )(
-        halves,
+        spectra,
         channel_valid.reshape(2, K),
         jnp.asarray(forward_table()),
         jnp.asarray(inverse_table(scale)),

time: 55 us -> 49.3 us (0.90)
  local copies, waits for them, and re-layouts: 4.24 us -> 0.66 us
  Pallas kernels: 50.5 us -> 48.5 us
    reshape x2 -> x0, local copies, waits for them, and re-layouts: 2.67 us -> none  [on_device(): spectra.reshape(2, CB, W, 2, K).transpose(3, 2, 0, 1, 4)]
    pallas_call x1, Pallas kernels: 50.5 us -> 48.5 us  [on_device(): pl.pallas_call(functools.partial(kernel, n_blk, n_frq), out_shape=pltpu.V...]
    unnamed x1, local copies, waits for them, and re-layouts: 1.57 us -> 0.66 us
where the time goes in v3:
time: 49.3 us; the launch traced here: 49.2 us
  Pallas kernels  48.5 us (98%)
  local copies, waits for them, and re-layouts  0.66 us (1%)
    pallas_call x1, Pallas kernels, on_device(): pl.pallas_call(functools.partial(kernel, n_blk, n_frq), out_shape=pltpu.V...  48.5 us

profile of v3, /device:TPU:1, one launch (start us, length us, event | category | flops | bytes accessed | tf_op | source)
XLA Modules:
  0.0 49.2 jit_solution(6928879460683005563)
XLA Ops:
  0.0 48.5 %shard_map.64 = f32[4,32,201]{2,1,0:T(8,128)S(1)} custom-call(bf16[2,256,4,256]{3,2,1,0:T(4,128)(2,1)} %raw_hbm.1, s32[2,128]{1,0:T(2,128)} %bitcast.5, bf16[768,512]{1,0:T(8,128)(2,1)} %constant.8.clone.fwd_hbm, bf16[512,768]{1,0:T(8,128)(2,1)} %constant.9.clone.inv_hbm, f32[2,128,256]{2,1,0:T(8,128)} %constant.10.clone.fine_hbm, ...), custom_call_target="tpu_custom_call" | custom-call | tf_op jit(solution)/shard_map/pallas_call | solution.py:314
  48.5 0.7 %copy.8 = f32[1,4,201,32]{2,3,1,0:T(8,128)} copy(f32[1,4,201,32]{2,3,1,0:T(8,128)S(1)} %bitcast.4) | data formatting | bytes 205824

commit v4 on v3

--- a/solution.py
+++ b/solution.py
@@ -17,14 +17,18 @@
 M = 384
 K = 128
 TAU = 256
-EARLY = 3
+PARTS = 4
+PART = CB // PARTS
+EARLY = 1
 MESH = pl.DeviceIdType.MESH
 
 
 def forward_table():
     angle = 2.0 * np.pi / M * (np.outer(np.arange(M), np.arange(CB)) % M)
     cos, sin = np.cos(angle), np.sin(angle)
-    return np.block([[cos, sin], [-sin, cos]]).astype(ml_dtypes.bfloat16)
+    table = np.block([[cos, sin], [-sin, cos]])
+    table = table.reshape(2 * M, 2, PARTS, PART).transpose(0, 2, 1, 3).reshape(2 * M, 2 * CB)
+    return table.astype(ml_dtypes.bfloat16)
 
 
 def inverse_table(scale):
@@ -54,9 +58,9 @@
 
 
 def kernel(
-    n_blk, n_frq, raw_hbm, valid_ref, fwd_hbm, inv_hbm, fine_hbm, coarse_hbm, out_ref,
-    raw, fwd, inv, fine, coarse, lag, column, mine, near, hats, acc, part_out, part_in, piece_out, piece_in,
-    load_sem, local_sem, send_sem, recv_sem, part_send, part_recv, piece_send, piece_recv, ready,
+    n_blk, n_frq, raw_hbm, valid_hbm, fwd_hbm, inv_hbm, fine_hbm, coarse_hbm, out_ref,
+    raw, valid, fwd, inv, fine, coarse, lag, column, mine, near, hats, acc, part_out, part_in, piece_out, piece_in,
+    load_sem, raw_sem, local_sem, send_sem, recv_sem, part_send, part_recv, piece_send, piece_recv, ready,
 ):
     blk = lax.axis_index("blk")
     frq = lax.axis_index("frq")
@@ -67,15 +71,20 @@
     left = (chip + chips - 1) % chips
     partner = (chip * 2 + 1 - core, frq)
 
+    def raw_load(part):
+        channels = pl.ds(part * PART, PART)
+        return pltpu.make_async_copy(raw_hbm.at[:, channels], raw.at[:, channels], raw_sem.at[part])
+
     loads = [
-        pltpu.make_async_copy(raw_hbm, raw, load_sem.at[0]),
-        pltpu.make_async_copy(fwd_hbm, fwd, load_sem.at[1]),
-        pltpu.make_async_copy(inv_hbm, inv, load_sem.at[2]),
-        pltpu.make_async_copy(fine_hbm, fine, load_sem.at[3]),
-        pltpu.make_async_copy(coarse_hbm.at[frq * 2 + core], coarse, load_sem.at[4]),
+        pltpu.make_async_copy(fwd_hbm, fwd, load_sem.at[0]),
+        pltpu.make_async_copy(inv_hbm, inv, load_sem.at[1]),
+        pltpu.make_async_copy(fine_hbm, fine, load_sem.at[2]),
+        pltpu.make_async_copy(coarse_hbm.at[frq * 2 + core], coarse, load_sem.at[3]),
     ]
-    for copy in loads:
-        copy.start()
+    valid_load = pltpu.make_async_copy(valid_hbm, valid, load_sem.at[4])
+    valid_load.start()
+    for part in range(PARTS):
+        raw_load(part).start()
 
     barrier = pltpu.get_barrier_semaphore()
     side = n_frq // 2
@@ -87,22 +96,22 @@
     for peer in peers:
         pl.semaphore_signal(barrier, inc=1, device_id=peer, device_id_type=MESH)
 
+    valid_load.wait()
     here = lax.broadcasted_iota(jnp.int32, (K, K), 0) == lax.broadcasted_iota(jnp.int32, (K, K), 1)
     for part in range(CB // K):
-        row = valid_ref[part : part + 1, :].astype(jnp.float32)
+        row = valid[part : part + 1, :].astype(jnp.float32)
         spread = jnp.where(here, jnp.broadcast_to(row, (K, K)), 0.0)
         total = jnp.sum(spread, axis=1, keepdims=True)
         column[part * K : (part + 1) * K] = jnp.broadcast_to(total, (K, K))
 
-    loads[0].wait()
-
-    def whiten(t, carry):
-        real = pl.ds(pl.multiple_of(t * 16, 16), 16)
-        imag = pl.ds(pl.multiple_of(CB + t * 16, 16), 16)
-        keep = column[real]
+    def whiten(part, t, carry):
+        channels = pl.ds(pl.multiple_of(part * PART + t * 16, 16), 16)
+        real = pl.ds(pl.multiple_of(2 * part * PART + t * 16, 16), 16)
+        imag = pl.ds(pl.multiple_of((2 * part + 1) * PART + t * 16, 16), 16)
+        keep = column[channels]
         for half in range(2):
             lanes = slice(half * K, (half + 1) * K)
-            both = [jnp.swapaxes(raw[r, real, :, lanes].astype(jnp.float32), 0, 1) for r in range(2)]
+            both = [jnp.swapaxes(raw[r, channels, :, lanes].astype(jnp.float32), 0, 1) for r in range(2)]
             values = [(both[0][w], both[1][w]) for w in range(W)]
             power = sum(re * re + im * im for re, im in values) * (1.0 / W)
             factor = keep / jnp.maximum(jnp.sqrt(power), 0.5)
@@ -111,9 +120,6 @@
                 mine[half, w, imag] = (im * factor).astype(jnp.bfloat16)
         return carry
 
-    lax.fori_loop(0, CB // 16, whiten, 0, unroll=2)
-    pl.semaphore_wait(barrier, len(peers))
-
     def local_copy(w):
         return pltpu.make_async_copy(mine.at[core, w], near.at[0, w, core], local_sem.at[w])
 
@@ -139,9 +145,31 @@
             device_id_type=MESH,
         )
 
+    def first_chunk(half, part):
+        chunk = pl.ds(2 * part * PART, 2 * PART)
+        return pltpu.make_async_remote_copy(
+            src_ref=mine.at[half, 0, chunk],
+            dst_ref=near.at[1, 0, 1 - core, chunk],
+            send_sem=send_sem.at[1, 0, half],
+            recv_sem=recv_sem.at[1, 0, 1 - core],
+            device_id=(jnp.where(core == 1, right, left) * 2 + half, frq),
+            device_id_type=MESH,
+        )
+
+    for part in range(PARTS):
+        raw_load(part).wait()
+        lax.fori_loop(0, PART // 16, functools.partial(whiten, part), 0, unroll=2)
+        if part == 0:
+            pl.semaphore_wait(barrier, len(peers))
+        for half in range(2):
+            first_chunk(half, part).start()
+        if part == 0:
+            for copy in loads:
+                copy.start()
     for w in range(W):
-        for half in range(2):
-            chip_copy(1, w, half).start()
+        if w > 0:
+            for half in range(2):
+                chip_copy(1, w, half).start()
         partner_copy(w).start()
         local_copy(w).start()
 
@@ -150,7 +178,7 @@
         pl.semaphore_wait(ready.at[step], 1)
 
     acc[...] = jnp.zeros_like(acc)
-    for copy in loads[1:]:
+    for copy in loads:
         copy.wait()
     fine_cos, fine_sin = fine[0], fine[1]
     coarse_cos, coarse_sin = coarse[0:1], coarse[1:2]
@@ -181,7 +209,7 @@
                 acc[phase - 1, index, im] += ai * br - ar * bi
             return carry
 
-        lax.fori_loop(0, M // 8, tile, 0, unroll=2)
+        lax.fori_loop(0, M // 8, tile, 0, unroll=16)
 
     def correlations(phase, index):
         both = jnp.concatenate([acc[phase - 1, index], acc[phase - 1, index + 1]], axis=1)
@@ -314,10 +342,11 @@
     stacked = pl.pallas_call(
         functools.partial(kernel, n_blk, n_frq),
         out_shape=pltpu.VMEM((ROUNDS, rows, LAGS), jnp.float32),
-        in_specs=[hbm, vmem, hbm, hbm, hbm, hbm],
+        in_specs=[hbm, hbm, hbm, hbm, hbm, hbm],
         out_specs=vmem,
         scratch_shapes=[
             pltpu.VMEM((2, CB, W, 2 * K), jnp.bfloat16),
+            pltpu.VMEM((2, K), jnp.int32),
             pltpu.VMEM((2 * M, 2 * CB), jnp.bfloat16),
             pltpu.VMEM((2 * CB, 2 * M), jnp.bfloat16),
             pltpu.VMEM((2, K, TAU), jnp.float32),
@@ -333,6 +362,7 @@
             pltpu.VMEM((2, 2, CB, TAU), jnp.bfloat16),
             pltpu.VMEM((ROUNDS, n_frq, rows, TAU), jnp.bfloat16),
             dma((5,)),
+            dma((PARTS,)),
             dma((W,)),
             dma((3, W, 2)),
             dma((3, W, 2)),

time: 49.3 us -> 47.6 us (0.966)
  Pallas kernels: 48.5 us -> 46.8 us
    pallas_call x1, Pallas kernels: 48.5 us -> 46.8 us  [on_device(): pl.pallas_call(functools.partial(kernel, n_blk, n_frq), out_shape=pltpu.V...]
where the time goes in v4:
time: 47.6 us; the launch traced here: 47.5 us
  Pallas kernels  46.8 us (98%)
  local copies, waits for them, and re-layouts  0.66 us (1%)
    pallas_call x1, Pallas kernels, on_device(): pl.pallas_call(functools.partial(kernel, n_blk, n_frq), out_shape=pltpu.V...  46.8 us

profile of v4, /device:TPU:1, one launch (start us, length us, event | category | flops | bytes accessed | tf_op | source)
XLA Modules:
  0.0 47.5 jit_solution(15839407995621625429)
XLA Ops:
  0.0 46.8 %shard_map.64 = f32[4,32,201]{2,1,0:T(8,128)S(1)} custom-call(bf16[2,256,4,256]{3,2,1,0:T(4,128)(2,1)} %raw_hbm.1, s32[2,128]{1,0:T(2,128)} %bitcast.5, bf16[768,512]{1,0:T(8,128)(2,1)} %constant.8.clone.fwd_hbm, bf16[512,768]{1,0:T(8,128)(2,1)} %constant.9.clone.inv_hbm, f32[2,128,256]{2,1,0:T(8,128)} %constant.10.clone.fine_hbm, ...), custom_call_target="tpu_custom_call" | custom-call | tf_op jit(solution)/shard_map/pallas_call | solution.py:342
  46.8 0.7 %copy.8 = f32[1,4,201,32]{2,3,1,0:T(8,128)} copy(f32[1,4,201,32]{2,3,1,0:T(8,128)S(1)} %bitcast.4) | data formatting | bytes 205824

commit v5 on v4

--- a/solution.py
+++ b/solution.py
@@ -215,10 +215,10 @@
         both = jnp.concatenate([acc[phase - 1, index], acc[phase - 1, index + 1]], axis=1)
         stack = jnp.dot(inv[...], both.astype(jnp.bfloat16), preferred_element_type=jnp.float32)
         stack = stack.astype(jnp.bfloat16)
-        for c in range(2):
+        for c in (1, 0):
             lanes = slice(c * K, (c + 1) * K)
             pair = jnp.concatenate([stack[:CB, lanes], stack[CB:, lanes]], axis=1)
-            yield jnp.dot(pair, lag[...], preferred_element_type=jnp.float32)
+            yield c, jnp.dot(pair, lag[...], preferred_element_type=jnp.float32)
 
     def part_copy(phase, i):
         return pltpu.make_async_remote_copy(
@@ -235,12 +235,15 @@
             return (0, 0) if i == 0 else (2 - core, 1 - core)
         return (1 + core, 0) if i == 0 else (3, 1)
 
+    order = [half_off * side + off_x for half_off in (1, 0) for off_x in (2, 1, 3, 0)][:-1]
+
     def piece_rows(other):
         return pl.ds(pl.multiple_of(other * rows, rows), rows)
 
     def piece_copy(phase, i, off):
         j, shift = place(phase, i)
-        other = (frq + off) % n_frq
+        half_off, off_x = divmod(off, side)
+        other = ((frq // side + half_off) % 2) * side + (frq + off_x) % side
         return pltpu.make_async_remote_copy(
             src_ref=piece_out.at[phase - 1, i, piece_rows(other)],
             dst_ref=piece_in.at[j, frq],
@@ -257,14 +260,14 @@
         )
 
     def scatter(phase):
-        for i, value in enumerate(correlations(phase, (1 - core) * 2)):
+        for i, value in correlations(phase, (1 - core) * 2):
             part_out[phase - 1, i] = value.astype(jnp.bfloat16)
             part_copy(phase, i).start()
-        for i, value in enumerate(correlations(phase, core * 2)):
+        for i, value in correlations(phase, core * 2):
             part_copy(phase, i).wait_recv()
             both = value + part_in[phase - 1, i].astype(jnp.float32)
             piece_out[phase - 1, i] = both.astype(jnp.bfloat16)
-            for off in range(1, n_frq):
+            for off in order:
                 piece_copy(phase, i, off).start()
             if i == 0:
                 own_copy(phase, i).start()

time: 47.6 us -> 47.1 us (0.989)
  no operation moved by 1% of the time
where the time goes in v5:
time: 47.1 us
  Pallas kernels  46.4 us (99%)
  local copies, waits for them, and re-layouts  0.66 us (1%)
    pallas_call x1, Pallas kernels, on_device(): pl.pallas_call(functools.partial(kernel, n_blk, n_frq), out_shape=pltpu.V...  46.4 us

profile of v5, /device:TPU:1, one launch (start us, length us, event | category | flops | bytes accessed | tf_op | source)
XLA Modules:
  0.0 47.1 jit_solution(5652914525015080690)
XLA Ops:
  0.0 46.4 %shard_map.64 = f32[4,32,201]{2,1,0:T(8,128)S(1)} custom-call(bf16[2,256,4,256]{3,2,1,0:T(4,128)(2,1)} %raw_hbm.1, s32[2,128]{1,0:T(2,128)} %bitcast.5, bf16[768,512]{1,0:T(8,128)(2,1)} %constant.8.clone.fwd_hbm, bf16[512,768]{1,0:T(8,128)(2,1)} %constant.9.clone.inv_hbm, f32[2,128,256]{2,1,0:T(8,128)} %constant.10.clone.fine_hbm, ...), custom_call_target="tpu_custom_call" | custom-call | tf_op jit(solution)/shard_map/pallas_call | solution.py:345
  46.4 0.7 %copy.8 = f32[1,4,201,32]{2,3,1,0:T(8,128)} copy(f32[1,4,201,32]{2,3,1,0:T(8,128)S(1)} %bitcast.4) | data formatting | bytes 205824

commit v6 on v5

--- a/solution.py
+++ b/solution.py
@@ -52,8 +52,8 @@
 
 C, D, B, E, A, F = (0, 0), (0, 1), (1, 0), (1, 1), (2, 0), (2, 1)
 PHASE_PAIRS = (
-    ((C, B), (E, B), (D, C), (D, B)),
-    ((C, A), (E, A), (D, A), (F, B)),
+    ((C, B), (E, B), (D, C), (D, B), (E, C)),
+    (None, (E, A), (D, A), (F, B)),
 )
 
 
@@ -194,7 +194,7 @@
 
     def cross(phase, w):
         pairs = PHASE_PAIRS[phase - 1]
-        used = sorted({block for pair in pairs for block in pair})
+        used = sorted({block for pair in pairs if pair for block in pair})
 
         def tile(t, carry):
             re = pl.ds(pl.multiple_of(t * 8, 8), 8)
@@ -203,22 +203,26 @@
             for slot, c in used:
                 lanes = slice(c * K, (c + 1) * K)
                 value[slot, c] = (hats[slot, w, re, lanes], hats[slot, w, im, lanes])
-            for index, (one, two) in enumerate(pairs):
-                (ar, ai), (br, bi) = value[one], value[two]
+            for index, pair in enumerate(pairs):
+                if pair is None:
+                    continue
+                (ar, ai), (br, bi) = value[pair[0]], value[pair[1]]
                 acc[phase - 1, index, re] += ar * br + ai * bi
                 acc[phase - 1, index, im] += ai * br - ar * bi
             return carry
 
         lax.fori_loop(0, M // 8, tile, 0, unroll=16)
 
-    def correlations(phase, index):
-        both = jnp.concatenate([acc[phase - 1, index], acc[phase - 1, index + 1]], axis=1)
+    def stacked_pairs(phase, index, count):
+        both = jnp.concatenate([acc[phase - 1, index + c] for c in range(count)], axis=1)
         stack = jnp.dot(inv[...], both.astype(jnp.bfloat16), preferred_element_type=jnp.float32)
         stack = stack.astype(jnp.bfloat16)
-        for c in (1, 0):
+        for c in reversed(range(count)):
             lanes = slice(c * K, (c + 1) * K)
-            pair = jnp.concatenate([stack[:CB, lanes], stack[CB:, lanes]], axis=1)
-            yield c, jnp.dot(pair, lag[...], preferred_element_type=jnp.float32)
+            yield c, jnp.concatenate([stack[:CB, lanes], stack[CB:, lanes]], axis=1)
+
+    def correlation(pair):
+        return jnp.dot(pair, lag[...], preferred_element_type=jnp.float32)
 
     def part_copy(phase, i):
         return pltpu.make_async_remote_copy(
@@ -232,7 +236,7 @@
 
     def place(phase, i):
         if phase == 1:
-            return (0, 0) if i == 0 else (2 - core, 1 - core)
+            return ((0, 0), (2 - core, 1 - core), (1, 1))[i]
         return (1 + core, 0) if i == 0 else (3, 1)
 
     order = [half_off * side + off_x for half_off in (1, 0) for off_x in (2, 1, 3, 0)][:-1]
@@ -259,11 +263,31 @@
             piece_out.at[phase - 1, i, piece_rows(frq)], piece_in.at[j, frq], piece_recv.at[j, frq]
         )
 
-    def scatter(phase):
-        for i, value in correlations(phase, (1 - core) * 2):
-            part_out[phase - 1, i] = value.astype(jnp.bfloat16)
+    def only(which):
+        def run(body):
+            if which is None:
+                body()
+            else:
+                pl.when(core == which)(body)
+
+        return run
+
+    def reducer(phase, i):
+        return {(1, 2): 0, (2, 0): 1}.get((phase, i))
+
+    def other_core(which):
+        return None if which is None else 1 - which
+
+    def give_part(phase, i, pair):
+        @only(other_core(reducer(phase, i)))
+        def _():
+            part_out[phase - 1, i] = correlation(pair).astype(jnp.bfloat16)
             part_copy(phase, i).start()
-        for i, value in correlations(phase, core * 2):
+
+    def give_pieces(phase, i, pair):
+        @only(reducer(phase, i))
+        def _():
+            value = correlation(pair)
             part_copy(phase, i).wait_recv()
             both = value + part_in[phase - 1, i].astype(jnp.float32)
             piece_out[phase - 1, i] = both.astype(jnp.bfloat16)
@@ -271,7 +295,7 @@
                 piece_copy(phase, i, off).start()
             if i == 0:
                 own_copy(phase, i).start()
-            elif phase == 2:
+            elif (phase, i) != (1, 1):
                 piece_copy(phase, i, 0).start()
             else:
                 @pl.when(core == 0)
@@ -281,6 +305,29 @@
                 @pl.when(core == 1)
                 def _():
                     own_copy(1, 1).start()
+
+    def scatter(phase):
+        if phase == 1:
+            @only(1)
+            def _():
+                for _, pair in stacked_pairs(1, 4, 1):
+                    part_out[0, 2] = correlation(pair).astype(jnp.bfloat16)
+                part_copy(1, 2).start()
+
+        for i, pair in stacked_pairs(phase, (1 - core) * 2, 2):
+            give_part(phase, i, pair)
+        for i, pair in stacked_pairs(phase, core * 2, 2):
+            give_pieces(phase, i, pair)
+        if phase == 1:
+            @only(0)
+            def _():
+                for _, pair in stacked_pairs(1, 4, 1):
+                    value = correlation(pair)
+                part_copy(1, 2).wait_recv()
+                both = value + part_in[0, 2].astype(jnp.float32)
+                piece_out[0, 2] = both.astype(jnp.bfloat16)
+                for off in order + [0]:
+                    piece_copy(1, 2, off).start()
 
     def first(w, carry):
         local_copy(w).wait()
@@ -322,12 +369,17 @@
         for half in range(2):
             chip_copy(1, w, half).wait_send()
             chip_copy(2, w, half).wait_send()
-    for phase in (1, 2):
-        for i in range(2):
+    for phase, i in ((1, 0), (1, 1), (1, 2), (2, 0), (2, 1)):
+        @only(other_core(reducer(phase, i)))
+        def _():
             part_copy(phase, i).wait_send()
-            for off in range(1, n_frq):
+
+        @only(reducer(phase, i))
+        def _():
+            for off in order:
                 piece_copy(phase, i, off).wait_send()
-    piece_copy(2, 1, 0).wait_send()
+            if (phase, i) in ((1, 2), (2, 1)):
+                piece_copy(phase, i, 0).wait_send()
 
     @pl.when(core == 0)
     def _():
@@ -359,19 +411,19 @@
             pltpu.VMEM((2, W, 2 * CB, K), jnp.bfloat16),
             pltpu.VMEM((3, W, 2, 2 * CB, K), jnp.bfloat16),
             pltpu.VMEM((3, W, 2 * M, 2 * K), jnp.float32),
-            pltpu.VMEM((2, ROUNDS, 2 * M, K), jnp.float32),
-            pltpu.VMEM((2, 2, CB, TAU), jnp.bfloat16),
-            pltpu.VMEM((2, 2, CB, TAU), jnp.bfloat16),
-            pltpu.VMEM((2, 2, CB, TAU), jnp.bfloat16),
+            pltpu.VMEM((2, 5, 2 * M, K), jnp.float32),
+            pltpu.VMEM((2, 3, CB, TAU), jnp.bfloat16),
+            pltpu.VMEM((2, 3, CB, TAU), jnp.bfloat16),
+            pltpu.VMEM((2, 3, CB, TAU), jnp.bfloat16),
             pltpu.VMEM((ROUNDS, n_frq, rows, TAU), jnp.bfloat16),
             dma((5,)),
             dma((PARTS,)),
             dma((W,)),
             dma((3, W, 2)),
             dma((3, W, 2)),
-            dma((2, 2)),
-            dma((2, 2)),
-            dma((2, 2, n_frq)),
+            dma((2, 3)),
+            dma((2, 3)),
+            dma((2, 3, n_frq)),
             dma((ROUNDS, n_frq)),
             pltpu.SemaphoreType.REGULAR((3,)),
         ],

time: 47.1 us -> 46.9 us (level)
  no operation moved by 1% of the time
where the time goes in v6:
time: 46.9 us; the launch traced here: 46.8 us
  Pallas kernels  46.1 us (98%)
  local copies, waits for them, and re-layouts  0.66 us (1%)
    pallas_call x1, Pallas kernels, on_device(): pl.pallas_call(functools.partial(kernel, n_blk, n_frq), out_shape=pltpu.V...  46.1 us

profile of v6, /device:TPU:1, one launch (start us, length us, event | category | flops | bytes accessed | tf_op | source)
XLA Modules:
  0.0 46.8 jit_solution(14353072814102431653)
XLA Ops:
  0.0 46.1 %shard_map.64 = f32[4,32,201]{2,1,0:T(8,128)S(1)} custom-call(bf16[2,256,4,256]{3,2,1,0:T(4,128)(2,1)} %raw_hbm.1, s32[2,128]{1,0:T(2,128)} %bitcast.5, bf16[768,512]{1,0:T(8,128)(2,1)} %constant.8.clone.fwd_hbm, bf16[512,768]{1,0:T(8,128)(2,1)} %constant.9.clone.inv_hbm, f32[2,128,256]{2,1,0:T(8,128)} %constant.10.clone.fine_hbm, ...), custom_call_target="tpu_custom_call" | custom-call | tf_op jit(solution)/shard_map/pallas_call | solution.py:397
  46.1 0.7 %copy.8 = f32[1,4,201,32]{2,3,1,0:T(8,128)} copy(f32[1,4,201,32]{2,3,1,0:T(8,128)S(1)} %bitcast.4) | data formatting | bytes 205824

commit v7 on v6

--- a/solution.py
+++ b/solution.py
@@ -70,6 +70,7 @@
     right = (chip + 1) % chips
     left = (chip + chips - 1) % chips
     partner = (chip * 2 + 1 - core, frq)
+    has_left, has_right = chip > 0, chip < chips - 1
 
     def raw_load(part):
         channels = pl.ds(part * PART, PART)
@@ -91,10 +92,14 @@
     next_x, last_x = frq // side * side + (frq + 1) % side, frq // side * side + (frq + side - 1) % side
     across = (frq + side) % n_frq
     peers = [partner, (blk, next_x), (blk, last_x), (blk, across)]
-    for c in range(2):
-        peers += [(right * 2 + c, frq), (left * 2 + c, frq)]
-    for peer in peers:
-        pl.semaphore_signal(barrier, inc=1, device_id=peer, device_id_type=MESH)
+
+    def greet(devices):
+        for device in devices:
+            pl.semaphore_signal(barrier, inc=1, device_id=device, device_id_type=MESH)
+
+    greet(peers)
+    pl.when(has_left)(lambda: greet([(left * 2 + c, frq) for c in range(2)]))
+    pl.when(has_right)(lambda: greet([(right * 2 + c, frq) for c in range(2)]))
 
     valid_load.wait()
     here = lax.broadcasted_iota(jnp.int32, (K, K), 0) == lax.broadcasted_iota(jnp.int32, (K, K), 1)
@@ -145,6 +150,10 @@
             device_id_type=MESH,
         )
 
+    def sends(phase):
+        rightward = core == (1 if phase == 1 else 0)
+        return (rightward & has_right) | (~rightward & has_left)
+
     def first_chunk(half, part):
         chunk = pl.ds(2 * part * PART, 2 * PART)
         return pltpu.make_async_remote_copy(
@@ -160,22 +169,38 @@
         raw_load(part).wait()
         lax.fori_loop(0, PART // 16, functools.partial(whiten, part), 0, unroll=2)
         if part == 0:
-            pl.semaphore_wait(barrier, len(peers))
-        for half in range(2):
-            first_chunk(half, part).start()
+            pl.semaphore_wait(
+                barrier, len(peers) + jnp.where(has_left, 2, 0) + jnp.where(has_right, 2, 0)
+            )
+        @pl.when(sends(1))
+        def _():
+            for half in range(2):
+                first_chunk(half, part).start()
+
         if part == 0:
             for copy in loads:
                 copy.start()
-    for w in range(W):
-        if w > 0:
+    @pl.when(sends(1))
+    def _():
+        for w in range(1, W):
             for half in range(2):
                 chip_copy(1, w, half).start()
+
+    for w in range(W):
         partner_copy(w).start()
         local_copy(w).start()
 
-    for step, target in enumerate([(blk, last_x), (blk, across), (left * 2 + core, frq)]):
+    for step, target in enumerate([(blk, last_x), (blk, across)]):
         pl.semaphore_signal(ready.at[step], inc=1, device_id=target, device_id_type=MESH)
         pl.semaphore_wait(ready.at[step], 1)
+
+    @pl.when(has_left)
+    def _():
+        pl.semaphore_signal(ready.at[2], inc=1, device_id=(left * 2 + core, frq), device_id_type=MESH)
+
+    @pl.when(has_right)
+    def _():
+        pl.semaphore_wait(ready.at[2], 1)
 
     acc[...] = jnp.zeros_like(acc)
     for copy in loads:
@@ -187,6 +212,10 @@
 
     def wait_landed(slot, w, c):
         pltpu.make_async_copy(near.at[slot, w, c], near.at[slot, w, c], recv_sem.at[slot, w, c]).wait()
+
+    def wait_sides(slot, w):
+        pl.when(has_left)(lambda: wait_landed(slot, w, 0))
+        pl.when(has_right)(lambda: wait_landed(slot, w, 1))
 
     def hat(slot, w):
         data = jnp.concatenate([near[slot, w, 0], near[slot, w, 1]], axis=1)
@@ -278,6 +307,30 @@
     def other_core(which):
         return None if which is None else 1 - which
 
+    def pieces(phase, i, act):
+        def away():
+            for off in order + [0]:
+                act(piece_copy(phase, i, off))
+
+        def here():
+            for off in order:
+                act(piece_copy(phase, i, off))
+
+        if i == 0:
+            here()
+        elif (phase, i) != (1, 1):
+            pl.when(has_right)(away)
+        else:
+            pl.when((core == 0) & has_right)(away)
+            pl.when(core == 1)(here)
+
+    def start_pieces(phase, i):
+        pieces(phase, i, lambda copy: copy.start())
+        if i == 0:
+            own_copy(phase, i).start()
+        elif (phase, i) == (1, 1):
+            pl.when(core == 1)(lambda: own_copy(1, 1).start())
+
     def give_part(phase, i, pair):
         @only(other_core(reducer(phase, i)))
         def _():
@@ -291,20 +344,7 @@
             part_copy(phase, i).wait_recv()
             both = value + part_in[phase - 1, i].astype(jnp.float32)
             piece_out[phase - 1, i] = both.astype(jnp.bfloat16)
-            for off in order:
-                piece_copy(phase, i, off).start()
-            if i == 0:
-                own_copy(phase, i).start()
-            elif (phase, i) != (1, 1):
-                piece_copy(phase, i, 0).start()
-            else:
-                @pl.when(core == 0)
-                def _():
-                    piece_copy(1, 1, 0).start()
-
-                @pl.when(core == 1)
-                def _():
-                    own_copy(1, 1).start()
+            start_pieces(phase, i)
 
     def scatter(phase):
         if phase == 1:
@@ -326,29 +366,30 @@
                 part_copy(1, 2).wait_recv()
                 both = value + part_in[0, 2].astype(jnp.float32)
                 piece_out[0, 2] = both.astype(jnp.bfloat16)
-                for off in order + [0]:
-                    piece_copy(1, 2, off).start()
+                start_pieces(1, 2)
 
     def first(w, carry):
         local_copy(w).wait()
         wait_landed(0, w, 1 - core)
         hat(0, w)
-        for c in range(2):
-            wait_landed(1, w, c)
+        wait_sides(1, w)
         hat(1, w)
         cross(1, w)
         return carry
 
     lax.fori_loop(0, EARLY, first, 0)
-    for w in range(W):
-        for half in range(2):
-            chip_copy(2, w, half).start()
+
+    @pl.when(sends(2))
+    def _():
+        for w in range(W):
+            for half in range(2):
+                chip_copy(2, w, half).start()
+
     lax.fori_loop(EARLY, W, first, 0)
     scatter(1)
 
     def second(w, carry):
-        for c in range(2):
-            wait_landed(2, w, c)
+        wait_sides(2, w)
         hat(2, w)
         cross(2, w)
         return carry
@@ -358,32 +399,33 @@
 
     for j in range(ROUNDS):
         total = jnp.zeros((rows, TAU), jnp.float32)
+        come = True if j == 0 else has_left if j == 3 else (core == 1) | has_left
+
+        @pl.when(come)
+        def _():
+            for f in range(n_frq):
+                pltpu.make_async_copy(piece_in.at[j, f], piece_in.at[j, f], piece_recv.at[j, f]).wait()
+
         for f in range(n_frq):
-            pltpu.make_async_copy(piece_in.at[j, f], piece_in.at[j, f], piece_recv.at[j, f]).wait()
             total += piece_in[j, f].astype(jnp.float32)
         total = jnp.where(blk > j, total, 0.0)
         out_ref[j] = total[:, :LAGS]
 
     for w in range(W):
         partner_copy(w).wait_send()
-        for half in range(2):
-            chip_copy(1, w, half).wait_send()
-            chip_copy(2, w, half).wait_send()
+    for phase in (1, 2):
+        @pl.when(sends(phase))
+        def _():
+            for w in range(W):
+                for half in range(2):
+                    chip_copy(phase, w, half).wait_send()
+
     for phase, i in ((1, 0), (1, 1), (1, 2), (2, 0), (2, 1)):
         @only(other_core(reducer(phase, i)))
         def _():
             part_copy(phase, i).wait_send()
 
-        @only(reducer(phase, i))
-        def _():
-            for off in order:
-                piece_copy(phase, i, off).wait_send()
-            if (phase, i) in ((1, 2), (2, 1)):
-                piece_copy(phase, i, 0).wait_send()
-
-    @pl.when(core == 0)
-    def _():
-        piece_copy(1, 1, 0).wait_send()
+        only(reducer(phase, i))(lambda: pieces(phase, i, lambda copy: copy.wait_send()))
 
 
 def on_device(n_blk, n_frq, spectra, channel_valid):

time: 46.9 us -> 46.4 us (0.989)
  the two profiles are of different devices: /device:TPU:1 before, /device:TPU:24 now
where the time goes in v7:
time: 46.4 us; the launch traced here: 46.3 us
  Pallas kernels  45.7 us (98%)
  local copies, waits for them, and re-layouts  0.66 us (1%)
    pallas_call x1, Pallas kernels, on_device(): pl.pallas_call(functools.partial(kernel, n_blk, n_frq), out_shape=pltpu.V...  45.7 us

profile of v7, /device:TPU:24, one launch (start us, length us, event | category | flops | bytes accessed | tf_op | source)
XLA Modules:
  0.0 46.3 jit_solution(3204392722122236256)
XLA Ops:
  0.0 45.7 %shard_map.64 = f32[4,32,201]{2,1,0:T(8,128)S(1)} custom-call(bf16[2,256,4,256]{3,2,1,0:T(4,128)(2,1)} %raw_hbm.1, s32[2,128]{1,0:T(2,128)} %bitcast.5, bf16[768,512]{1,0:T(8,128)(2,1)} %constant.8.clone.fwd_hbm, bf16[512,768]{1,0:T(8,128)(2,1)} %constant.9.clone.inv_hbm, f32[2,128,256]{2,1,0:T(8,128)} %constant.10.clone.fine_hbm, ...), custom_call_target="tpu_custom_call" | custom-call | tf_op jit(solution)/shard_map/pallas_call | solution.py:439
  45.7 0.7 %copy.8 = f32[1,4,201,32]{2,3,1,0:T(8,128)} copy(f32[1,4,201,32]{2,3,1,0:T(8,128)S(1)} %bitcast.4) | data formatting | bytes 205824

commit v8 on v7

--- a/solution.py
+++ b/solution.py
@@ -17,7 +17,7 @@
 M = 384
 K = 128
 TAU = 256
-PARTS = 4
+PARTS = 2
 PART = CB // PARTS
 EARLY = 1
 MESH = pl.DeviceIdType.MESH

time: 46.4 us -> 45.9 us (0.989)
  Pallas kernels: 45.7 us -> 45.1 us
    pallas_call x1, Pallas kernels: 45.7 us -> 45.1 us  [on_device(): pl.pallas_call(functools.partial(kernel, n_blk, n_frq), out_shape=pltpu.V...]
where the time goes in v8:
time: 45.9 us; the launch traced here: 45.8 us
  Pallas kernels  45.1 us (98%)
  local copies, waits for them, and re-layouts  0.66 us (1%)
    pallas_call x1, Pallas kernels, on_device(): pl.pallas_call(functools.partial(kernel, n_blk, n_frq), out_shape=pltpu.V...  45.1 us

profile of v8, /device:TPU:24, one launch (start us, length us, event | category | flops | bytes accessed | tf_op | source)
XLA Modules:
  0.0 45.8 jit_solution(10677986225229590811)
XLA Ops:
  0.0 45.1 %shard_map.64 = f32[4,32,201]{2,1,0:T(8,128)S(1)} custom-call(bf16[2,256,4,256]{3,2,1,0:T(4,128)(2,1)} %raw_hbm.1, s32[2,128]{1,0:T(2,128)} %bitcast.5, bf16[768,512]{1,0:T(8,128)(2,1)} %constant.8.clone.fwd_hbm, bf16[512,768]{1,0:T(8,128)(2,1)} %constant.9.clone.inv_hbm, f32[2,128,256]{2,1,0:T(8,128)} %constant.10.clone.fine_hbm, ...), custom_call_target="tpu_custom_call" | custom-call | tf_op jit(solution)/shard_map/pallas_call | solution.py:439
  45.1 0.7 %copy.8 = f32[1,4,201,32]{2,3,1,0:T(8,128)} copy(f32[1,4,201,32]{2,3,1,0:T(8,128)S(1)} %bitcast.4) | data formatting | bytes 205824

commit v9 on v8

--- a/solution.py
+++ b/solution.py
@@ -20,6 +20,7 @@
 PARTS = 2
 PART = CB // PARTS
 EARLY = 1
+LATER = 2
 MESH = pl.DeviceIdType.MESH
 
 
@@ -377,15 +378,18 @@
         cross(1, w)
         return carry
 
+    def send_second(windows):
+        @pl.when(sends(2))
+        def _():
+            for w in windows:
+                for half in range(2):
+                    chip_copy(2, w, half).start()
+
     lax.fori_loop(0, EARLY, first, 0)
-
-    @pl.when(sends(2))
-    def _():
-        for w in range(W):
-            for half in range(2):
-                chip_copy(2, w, half).start()
-
-    lax.fori_loop(EARLY, W, first, 0)
+    send_second(range(1))
+    lax.fori_loop(EARLY, LATER, first, 0)
+    send_second(range(1, W))
+    lax.fori_loop(LATER, W, first, 0)
     scatter(1)
 
     def second(w, carry):

time: 45.9 us -> 45.9 us (level)
  no operation moved by 1% of the time
where the time goes in v9:
time: 45.9 us; the launch traced here: 45.8 us
  Pallas kernels  45.1 us (98%)
  local copies, waits for them, and re-layouts  0.66 us (1%)
    pallas_call x1, Pallas kernels, on_device(): pl.pallas_call(functools.partial(kernel, n_blk, n_frq), out_shape=pltpu.V...  45.1 us

profile of v9, /device:TPU:24, one launch (start us, length us, event | category | flops | bytes accessed | tf_op | source)
XLA Modules:
  0.0 45.8 jit_solution(1645580690510794620)
XLA Ops:
  0.0 45.1 %shard_map.64 = f32[4,32,201]{2,1,0:T(8,128)S(1)} custom-call(bf16[2,256,4,256]{3,2,1,0:T(4,128)(2,1)} %raw_hbm.1, s32[2,128]{1,0:T(2,128)} %bitcast.5, bf16[768,512]{1,0:T(8,128)(2,1)} %constant.8.clone.fwd_hbm, bf16[512,768]{1,0:T(8,128)(2,1)} %constant.9.clone.inv_hbm, f32[2,128,256]{2,1,0:T(8,128)} %constant.10.clone.fine_hbm, ...), custom_call_target="tpu_custom_call" | custom-call | tf_op jit(solution)/shard_map/pallas_call | solution.py:443
  45.1 0.7 %copy.8 = f32[1,4,201,32]{2,3,1,0:T(8,128)} copy(f32[1,4,201,32]{2,3,1,0:T(8,128)S(1)} %bitcast.4) | data formatting | bytes 205824

commit v10 on v9

--- a/solution.py
+++ b/solution.py
@@ -20,7 +20,7 @@
 PARTS = 2
 PART = CB // PARTS
 EARLY = 1
-LATER = 2
+LATER = 3
 MESH = pl.DeviceIdType.MESH
 
 

time: 45.9 us -> 46.1 us (level)
  no operation moved by 1% of the time
where the time goes in v10:
time: 46.1 us; the launch traced here: 46 us
  Pallas kernels  45.3 us (98%)
  local copies, waits for them, and re-layouts  0.66 us (1%)
    pallas_call x1, Pallas kernels, on_device(): pl.pallas_call(functools.partial(kernel, n_blk, n_frq), out_shape=pltpu.V...  45.3 us

profile of v10, /device:TPU:24, one launch (start us, length us, event | category | flops | bytes accessed | tf_op | source)
XLA Modules:
  0.0 46.0 jit_solution(9824524807518486934)
XLA Ops:
  0.0 45.3 %shard_map.64 = f32[4,32,201]{2,1,0:T(8,128)S(1)} custom-call(bf16[2,256,4,256]{3,2,1,0:T(4,128)(2,1)} %raw_hbm.1, s32[2,128]{1,0:T(2,128)} %bitcast.5, bf16[768,512]{1,0:T(8,128)(2,1)} %constant.8.clone.fwd_hbm, bf16[512,768]{1,0:T(8,128)(2,1)} %constant.9.clone.inv_hbm, f32[2,128,256]{2,1,0:T(8,128)} %constant.10.clone.fine_hbm, ...), custom_call_target="tpu_custom_call" | custom-call | tf_op jit(solution)/shard_map/pallas_call | solution.py:443
  45.3 0.7 %copy.8 = f32[1,4,201,32]{2,3,1,0:T(8,128)} copy(f32[1,4,201,32]{2,3,1,0:T(8,128)S(1)} %bitcast.4) | data formatting | bytes 205824
